TPU v7x, 128 devices: a whole 4x4x4 slice. The times are simulated.
128 devices in a mesh: dp: 8 (over z, core), mp: 16 (over y, x).
Axes of the slice: x: 4, y: 4, z: 4, core: 2. Of those that a mesh axis runs over, the one named last changes fastest.
Arguments:
- acts: bfloat16 [1024, 8192], P('dp', 'mp'), may hold values from -6 to 6
- w_up: bfloat16 [8192, 14336], P(None, 'mp'), may hold values from -0.0625 to 0.0625
- out_grad: bfloat16 [1024, 14336], P('dp', 'mp'), may hold values from -6 to 6
- rotation: float32 [8192, 8192], P('mp', 'dp'), may hold values from -6 to 6
Outputs:
- half_rotation: float32 [8192, 8192], P('mp', 'dp')
- next_rotation: float32 [8192, 8192], P('mp', 'dp')
All inputs are finite; a program needn't handle non-finite values.
Results may differ from a plain program's by a relative error of at most 0.017.
Values may be sent and summed in bfloat16 or wider, within the bound.
A program may use at most 128 MiB of HBM per device.

v0:
```python
import functools
import math

import jax
import jax.numpy as jnp
from jax import lax
from jax.sharding import Mesh
from jax.sharding import PartitionSpec as P

D = 8192
ITERS = 2
DP = ("dp_0", "dp_1")
MP = ("mp_0", "mp_1")
DP_MP = ("dp_0", "dp_1", "mp_0", "mp_1")


step_gain = 0.5
epsilon = 1e-06


def by_axis(value, axes):
    return functools.reduce(lax.psum, axes, value)


def in_one_piece(arrays, axis, dim, along):
    both = jnp.concatenate(arrays, axis=along)
    filled, at, gathered = (lax.all_gather(both, axis, axis=dim, tiled=True), 0, [])
    for a in arrays:
        gathered.append(lax.slice_in_dim(filled, at, at + a.shape[along], axis=along))
        at += a.shape[along]
    return tuple(gathered)


def settle(term):
    return lax.optimization_barrier(term.astype(jnp.bfloat16)).astype(jnp.float32)


def contract_cols(left, right):
    return lax.dot_general(
        left, right, (((1,), (1,)), ((), ())), preferred_element_type=jnp.float32
    )


def local(acts, w_up, out_grad, rotation):
    inv_root = D ** (-0.5)
    rot_half = rotation.astype(jnp.bfloat16)
    rot_rows = lax.all_gather(rot_half, DP, axis=1, tiled=True)
    mixed = lax.psum(
        (jnp.dot(acts, rot_rows, preferred_element_type=jnp.float32) * inv_root).astype(
            jnp.bfloat16
        ),
        MP,
    )
    hidden = jnp.dot(mixed, w_up, preferred_element_type=jnp.float32)
    sigmoid_hidden = jax.nn.sigmoid(hidden)
    grad_hidden = (
        out_grad.astype(jnp.float32) * sigmoid_hidden * (1.0 + hidden * (1.0 - sigmoid_hidden))
    ).astype(jnp.bfloat16)
    grad_mixed = lax.psum(contract_cols(grad_hidden, w_up).astype(jnp.bfloat16), MP)
    factor = contract_cols(grad_mixed, rot_rows).astype(jnp.bfloat16)
    act_norm, factor_norm = (
        by_axis(jnp.sum(jnp.square(acts.astype(jnp.float32))), DP_MP),
        by_axis(jnp.sum(jnp.square(factor.astype(jnp.float32))), DP_MP),
    )
    token_count = acts.shape[0] * lax.axis_size(DP)
    spread = (token_count ** (-0.5) + D ** (-0.5)) ** 2
    step_size = (
        step_gain
        * math.sqrt(D)
        / (jnp.sqrt((act_norm + epsilon) * (factor_norm + epsilon)) * spread)
    )
    every_acts, every_factor = in_one_piece((acts, factor), DP, 0, 1)
    groups = lax.axis_size(DP)
    block_rows = acts.shape[0]
    acts_blocks = every_acts.reshape(groups, block_rows, -1)
    factor_blocks = every_factor.reshape(groups, block_rows, -1)
    current = rotation
    first_iterate = rotation
    for iteration in range(ITERS):
        point = (rotation + current).astype(jnp.bfloat16)
        left_sum, right_sum = (
            lax.psum(
                (
                    jnp.dot(every_factor, point, preferred_element_type=jnp.float32) * inv_root
                ).astype(jnp.bfloat16),
                MP,
            ).astype(jnp.float32),
            lax.psum(
                (jnp.dot(every_acts, point, preferred_element_type=jnp.float32) * inv_root).astype(
                    jnp.bfloat16
                ),
                MP,
            ).astype(jnp.float32),
        )
        left = left_sum.astype(jnp.bfloat16).reshape(groups, block_rows, -1)
        right = right_sum.astype(jnp.bfloat16).reshape(groups, block_rows, -1)
        terms = jnp.einsum(
            "ntr,ntc->nrc", acts_blocks, left, preferred_element_type=jnp.float32
        ) - jnp.einsum("ntr,ntc->nrc", factor_blocks, right, preferred_element_type=jnp.float32)
        update = jnp.sum(settle(terms), axis=0)
        current = rotation - step_size * update
        if iteration == 0:
            first_iterate = current
    return (first_iterate, current)


def solution(mesh):
    finer = Mesh(mesh.devices.reshape(4, 2, 4, 4), ("dp_0", "dp_1", "mp_0", "mp_1"))
    placed = (P(DP, MP), P(None, MP), P(DP, MP), P(MP, DP))
    return jax.shard_map(
        local, mesh=finer, in_specs=placed, out_specs=(P(MP, DP), P(MP, DP)), check_vma=False
    )
```

profile of v0, /device:TPU:1, one launch (start us, length us, event | category | flops | bytes accessed | tf_op | source)
XLA Modules:
  0.0 586.6 jit_solution(2937792211861183039)
XLA Ops:
  7.2 0.0 copy-start.7
  7.2 0.0 all-gather.3.cloned.1.call-start
  7.2 2.8 convert_element_type.64
  10.0 0.0 all-gather.3.cloned.1.call-update
  10.0 0.0 all-reduce.11.cloned.1.call-start
  10.0 53.8 %all-gather.3.cloned.1.call-done = bf16[512,8192]{1,0:T(8,128)(2,1)} async-done(((bf16[512,1024]{1,0:T(8,128)(2,1)}), bf16[512,8192]{1,0:T(8,128)(2,1)}) %all-gather.3.cloned.1.call-update) | async-done | bytes 8388624 | tf_op jit(solution)/shard_map/all_gather | solution.py:47
  63.8 0.0 copy-done.7
  63.8 6.0 %fusion = bf16[128,8192]{1,0:T(8,128)(2,1)} fusion(bf16[128,512]{1,0:T(8,128)(2,1)S(1)} %copy-done.7, bf16[512,8192]{1,0:T(8,128)(2,1)} %all-gather.3.cloned.1.call-done), kind=kOutput, calls=%fused_computation.5 | convolution fusion | flops 1075838976 | bytes 10616832 | tf_op jit(solution)/shard_map/dot_general | solution.py:49
  69.9 0.0 all-reduce.11.cloned.1.call-update
  69.9 0.0 all-reduce.13.cloned.1.call-start
  69.9 88.7 %all-reduce.11.cloned.1.call-done = bf16[128,8192]{1,0:T(8,128)(2,1)} async-done(((bf16[128,8192]{1,0:T(8,128)(2,1)}), bf16[128,8192]{1,0:T(8,128)(2,1)}) %all-reduce.11.cloned.1.call-update) | async-done | bytes 2097168 | tf_op jit(solution)/shard_map/psum | solution.py:48
  158.6 0.0 copy-done.8
  158.6 20.2 %convolution_convert_fusion = bf16[128,8192]{1,0:T(8,128)(2,1)} fusion(bf16[8192,896]{1,0:T(8,128)(2,1)} %param.5, bf16[128,896]{1,0:T(8,128)(2,1)S(1)} %copy-done.8, bf16[128,8192]{1,0:T(8,128)(2,1)} %all-reduce.11.cloned.1.call-done), kind=kOutput, calls=%fused_computation.6 | convolution fusion | flops 3760291840 | bytes 19103744 | tf_op jit(solution)/shard_map/dot_general | solution.py:39
  178.8 0.0 all-reduce.13.cloned.1.call-update
  178.8 0.0 copy-start
  178.8 0.0 all-gather.5.cloned.1.call-start
  178.9 89.5 %all-reduce.13.cloned.1.call-done = bf16[128,8192]{1,0:T(8,128)(2,1)} async-done(((bf16[128,8192]{1,0:T(8,128)(2,1)}), bf16[128,8192]{1,0:T(8,128)(2,1)}) %all-reduce.13.cloned.1.call-update) | async-done | bytes 2097168 | tf_op jit(solution)/shard_map/psum | solution.py:59
  268.4 7.7 %multiply_reduce_fusion = (f32[]{:T(128)}, bf16[128,512]{1,0:T(8,128)(2,1)S(1)}) fusion(bf16[128,8192]{1,0:T(8,128)(2,1)} %all-reduce.13.cloned.1.call-done, bf16[512,8192]{1,0:T(8,128)(2,1)} %all-gather.3.cloned.1.call-done), kind=kOutput, calls=%fused_computation.18 | convolution fusion | flops 1074003968 | bytes 10616836 | tf_op jit(solution)/shard_map/dot_general | solution.py:39
  276.1 0.7 pad_maximum_fusion
  276.8 0.0 all-gather.5.cloned.1.call-update
  276.8 0.0 all-reduce.17.cloned.1.call-start
  276.9 26.4 %all-gather.5.cloned.1.call-done = bf16[1024,1024]{1,0:T(8,128)(2,1)} async-done(((bf16[128,1024]{1,0:T(8,128)(2,1)}), bf16[1024,1024]{1,0:T(8,128)(2,1)}) %all-gather.5.cloned.1.call-update) | async-done | bytes 2097168 | tf_op jit(solution)/shard_map/all_gather | solution.py:27
  303.3 0.0 copy-done
  303.3 4.0 multiply_convert_fusion.3
  307.2 0.0 copy-done.5
  307.2 2.6 multiply_convert_fusion.2
  309.8 0.0 all-reduce.17.cloned.1.call-update
  309.8 0.0 all-reduce.15.cloned.1.call-start
  309.9 0.7 multiply_reduce_fusion.1
  310.6 7.9 %all-reduce.2 = (f32[]{:T(128)}, f32[]{:T(128)}) all-reduce(f32[]{:T(128)} %multiply_reduce_fusion.1, f32[]{:T(128)} %get-tuple-element.18), channel_id=1, replica_groups=mesh['dp_0'=4,'dp_1'=2,'mp_0'=4,'mp_1'=4] {'dp_0'}, use_global_device_ids=true, to_apply=%region_1.0 | all-reduce | flops 2 | bytes 16 | tf_op jit(solution)/shard_map/psum | solution.py:22
  318.5 5.1 all-reduce.3
  323.6 9.9 %all-reduce.1 = (f32[]{:T(128)}, f32[]{:T(128)}) all-reduce(f32[]{:T(128)} %get-tuple-element.8, f32[]{:T(128)} %get-tuple-element.9), channel_id=1, replica_groups=mesh['dp_0'=4,'dp_1'=2,'mp_0'=4,'mp_1'=4] {'mp_0'}, use_global_device_ids=true, to_apply=%region_3.0 | all-reduce | flops 2 | bytes 16 | tf_op jit(solution)/shard_map/psum | solution.py:22
  333.5 9.3 %all-reduce = (f32[]{:T(128)}, f32[]{:T(128)}) all-reduce(f32[]{:T(128)} %get-tuple-element.4, f32[]{:T(128)} %get-tuple-element.5), channel_id=1, replica_groups=mesh['dp_0'=4,'dp_1'=2,'mp_0'=4,'mp_1'=4] {'mp_1'}, use_global_device_ids=true, to_apply=%region_4.0 | all-reduce | flops 2 | bytes 16 | tf_op jit(solution)/shard_map/psum | solution.py:22
  344.2 2.6 fusion.7
  346.9 66.5 %all-reduce.17.cloned.1.call-done = (bf16[8,128,1024]{2,1,0:T(8,128)(2,1)}, bf16[8,128,1024]{2,1,0:T(8,128)(2,1)}) async-done(((bf16[8,128,1024]{2,1,0:T(8,128)(2,1)}, bf16[8,128,1024]{2,1,0:T(8,128)(2,1)}), (bf16[8,128,1024]{2,1,0:T(8,128)(2,1)}, bf16[8,128,1024]{2,1,0:T(8,128)(2,1)})) %all-reduce.17.cloned.1.call-update) | async-done | bytes 4194320 | tf_op jit(solution)/shard_map/psum | solution.py:82
  413.4 9.8 %fusion.10 = f32[8,512,1024]{2,1,0:T(8,128)} fusion(bf16[8,128,512]{2,1,0:T(8,128)(2,1)S(1)} %bitcast.23, bf16[8,128,1024]{2,1,0:T(8,128)(2,1)} %get-tuple-element.12), kind=kOutput, calls=%fused_computation.28 | convolution fusion | flops 1073741824 | bytes 19922944 | tf_op jit(solution)/shard_map/ntr,ntc->nrc/dot_general | solution.py:97
  423.2 0.0 copy-done.1
  423.2 11.4 %subtract_convert_fusion.1 = bf16[8,512,1024]{2,1,0:T(8,128)(2,1)} fusion(f32[8,512,1024]{2,1,0:T(8,128)} %fusion.10, bf16[8,128,512]{2,1,0:T(8,128)(2,1)S(1)} %bitcast.25, bf16[8,128,1024]{2,1,0:T(8,128)(2,1)S(1)} %copy-done.3), kind=kOutput, calls=%fused_computation.3 | convolution fusion | flops 1082130432 | bytes 28311552 | tf_op jit(solution)/shard_map/ntr,ntc->nrc/dot_general | solution.py:99
  434.6 5.7 convert_reduce_fusion.1
  440.3 1.8 add_convert_fusion
  442.2 2.6 multiply_convert_fusion
  444.8 2.6 multiply_convert_fusion.1
  447.4 0.0 all-reduce.15.cloned.1.call-update
  447.4 103.4 %all-reduce.15.cloned.1.call-done = (bf16[8,128,1024]{2,1,0:T(8,128)(2,1)}, bf16[8,128,1024]{2,1,0:T(8,128)(2,1)}) async-done(((bf16[8,128,1024]{2,1,0:T(8,128)(2,1)}, bf16[8,128,1024]{2,1,0:T(8,128)(2,1)}), (bf16[8,128,1024]{2,1,0:T(8,128)(2,1)}, bf16[8,128,1024]{2,1,0:T(8,128)(2,1)})) %all-reduce.15.cloned.1.call-update) | async-done | bytes 4194320 | tf_op jit(solution)/shard_map/psum | solution.py:82
  550.8 9.8 %fusion.11 = f32[8,512,1024]{2,1,0:T(8,128)} fusion(bf16[8,128,512]{2,1,0:T(8,128)(2,1)S(1)} %bitcast.24, bf16[8,128,1024]{2,1,0:T(8,128)(2,1)} %get-tuple-element.10), kind=kOutput, calls=%fused_computation.29 | convolution fusion | flops 1073741824 | bytes 19922944 | tf_op jit(solution)/shard_map/ntr,ntc->nrc/dot_general | solution.py:97
  560.7 11.7 %subtract_convert_fusion = bf16[8,512,1024]{2,1,0:T(8,128)(2,1)} fusion(f32[8,512,1024]{2,1,0:T(8,128)} %fusion.11, bf16[8,128,512]{2,1,0:T(8,128)(2,1)S(1)} %bitcast.26, bf16[8,128,1024]{2,1,0:T(8,128)(2,1)S(1)} %copy-done.4), kind=kOutput, calls=%fused_computation.1 | convolution fusion | flops 1082130432 | bytes 28311552 | tf_op jit(solution)/shard_map/ntr,ntc->nrc/dot_general | solution.py:99
  572.3 5.7 convert_reduce_fusion
  578.0 1.8 multiply_subtract_fusion
  (11 shorter events, 0.0 us)
Async XLA Ops:
  7.2 56.7 %copy-start.7 = (bf16[128,512]{1,0:T(8,128)(2,1)S(1)}, bf16[128,512]{1,0:T(8,128)(2,1)}, u32[]{:S(2)}) copy-start(bf16[128,512]{1,0:T(8,128)(2,1)} %param.4) | copy-start | bytes 393220
  7.2 56.7 %all-gather.3.cloned.1.call-start = ((), (), s32[]{:S(2)}) async-start(), calls=%async_computation | async-start | bytes 9437184 | tf_op jit(solution)/shard_map/all_gather | solution.py:47
  10.0 148.6 %all-reduce.11.cloned.1.call-start = ((), (), s32[]{:S(2)}) async-start(), calls=%async_computation.1 | async-start | bytes 4194304 | tf_op jit(solution)/shard_map/psum | solution.py:48
  69.9 88.8 %copy-start.8 = (bf16[128,896]{1,0:T(8,128)(2,1)S(1)}, bf16[128,896]{1,0:T(8,128)(2,1)}, u32[]{:S(2)}) copy-start(bf16[128,896]{1,0:T(8,128)(2,1)} %param.6) | copy-start | bytes 688132
  69.9 198.5 %all-reduce.13.cloned.1.call-start = ((), (), s32[]{:S(2)}) async-start(), calls=%async_computation.2 | async-start | bytes 4194304 | tf_op jit(solution)/shard_map/psum | solution.py:59
  178.8 124.4 %copy-start = (f32[512,1024]{1,0:T(8,128)S(1)}, f32[512,1024]{1,0:T(8,128)}, u32[]{:S(2)}) copy-start(f32[512,1024]{1,0:T(8,128)} %param.7) | copy-start | bytes 6291460
  178.8 124.4 %all-gather.5.cloned.1.call-start = ((), (), s32[]{:S(2)}) async-start(), calls=%async_computation.3 | async-start | bytes 2359296 | tf_op jit(solution)/shard_map/all_gather | solution.py:27
  276.8 136.5 %all-reduce.17.cloned.1.call-start = ((), (), s32[]{:S(2)}) async-start(), calls=%async_computation.5 | async-start | bytes 8388608 | tf_op jit(solution)/shard_map/psum | solution.py:82
  303.3 4.0 copy-start.5
  309.8 241.0 %all-reduce.15.cloned.1.call-start = ((), (), s32[]{:S(2)}) async-start(), calls=%async_computation.4 | async-start | bytes 8388608 | tf_op jit(solution)/shard_map/psum | solution.py:82
  413.4 9.8 %copy-start.1 = (bf16[1024,512]{1,0:T(8,128)(2,1)S(1)}, bf16[1024,512]{1,0:T(8,128)(2,1)}, u32[]{:S(2)}) copy-start(bf16[1024,512]{1,0:T(8,128)(2,1)} %get-tuple-element.16) | copy-start | bytes 3145732
  413.4 9.8 %copy-start.3 = (bf16[8,128,1024]{2,1,0:T(8,128)(2,1)S(1)}, bf16[8,128,1024]{2,1,0:T(8,128)(2,1)}, u32[]{:S(2)}) copy-start(bf16[8,128,1024]{2,1,0:T(8,128)(2,1)} %get-tuple-element.13) | copy-start | bytes 6291460
  440.3 1.9 copy-start.6
  550.8 9.8 %copy-start.2 = (bf16[1024,512]{1,0:T(8,128)(2,1)S(1)}, bf16[1024,512]{1,0:T(8,128)(2,1)}, u32[]{:S(2)}) copy-start(bf16[1024,512]{1,0:T(8,128)(2,1)} %get-tuple-element.16) | copy-start | bytes 3145732
  550.8 9.8 %copy-start.4 = (bf16[8,128,1024]{2,1,0:T(8,128)(2,1)S(1)}, bf16[8,128,1024]{2,1,0:T(8,128)(2,1)}, u32[]{:S(2)}) copy-start(bf16[8,128,1024]{2,1,0:T(8,128)(2,1)} %get-tuple-element.11) | copy-start | bytes 6291460
Sparse Core Ops, SparseCore 0:
  10.3 53.5 all-gather.2
  70.0 88.5 all-reduce.10
  178.9 89.4 all-reduce.12
  276.9 26.2 all-gather.4
  310.0 103.3 all-reduce.16
  447.5 103.2 all-reduce.14
where the time goes:
time: 587 us
  waiting for transfers between devices  428 us (73%)
  matrix products  88.4 us (15%)
  blocking collectives  32.2 us (5%)
  other arithmetic  19.1 us (3%)
  between operations  15.6 us (3%)
    psum x2, waiting for transfers between devices, local(): lax.psum((jnp.dot(every_factor, point, preferred_element_type=jnp.float32...  170 us
    psum x1, waiting for transfers between devices, local(): lax.psum(contract_cols(grad_hidden, w_up).astype(jnp.bfloat16), MP)  89.5 us
    psum x1, waiting for transfers between devices, local(): lax.psum((jnp.dot(acts, rot_rows, preferred_element_type=jnp.float32) * i...  88.7 us
    all_gather x1, waiting for transfers between devices, local(): rot_rows = lax.all_gather(rot_half, DP, axis=1, tiled=True)  53.8 us
    psum x4, blocking collectives, by_axis(): return functools.reduce(lax.psum, axes, value)  32.2 us
    dot_general x2, matrix products, contract_cols(): lax.dot_general(left, right, (((1,), (1,)), ((), ())), preferred_element_...  27.8 us
    all_gather x1, waiting for transfers between devices, in_one_piece(): lax.all_gather(both, axis, axis=dim, tiled=True)  26.4 us
    dot_general x2, matrix products, local(): jnp.einsum('ntr,ntc->nrc', factor_blocks, right, preferred_element_type=j...  23.1 us
  transfers between devices with their start and end apart: 6, of which 6 were waited for; matrix products, arithmetic and copies ran while one was open for 1% of the time, Pallas kernels for 0%

commit v1 on v0

v1 whole, which is shorter than its diff:
```python
import math

import jax
import jax.numpy as jnp
from jax import lax
from jax.sharding import PartitionSpec as P

D = 8192
step_gain = 0.5
epsilon = 1e-06


def contract_cols(left, right):
    return lax.dot_general(
        left, right, (((1,), (1,)), ((), ())), preferred_element_type=jnp.float32
    )


def contract_rows(left, right):
    return lax.dot_general(
        left, right, (((0,), (0,)), ((), ())), preferred_element_type=jnp.float32
    )


def local(acts, w_up, out_grad, rotation):
    inv_root = D ** (-0.5)
    rows = acts.shape[0]
    me = lax.axis_index("dp")
    tokens = rows * lax.axis_size("dp")
    rot_half = rotation.astype(jnp.bfloat16)
    rot_rows = lax.all_gather(rot_half, "dp", axis=1, tiled=True)
    acts_all = lax.all_gather(acts, "dp", axis=0, tiled=True)
    mixed = lax.psum(
        (jnp.dot(acts, rot_rows, preferred_element_type=jnp.float32) * inv_root).astype(
            jnp.bfloat16
        ),
        "mp",
    )
    hidden = jnp.dot(mixed, w_up, preferred_element_type=jnp.float32)
    sigmoid_hidden = jax.nn.sigmoid(hidden)
    grad_hidden = (
        out_grad.astype(jnp.float32) * sigmoid_hidden * (1.0 + hidden * (1.0 - sigmoid_hidden))
    ).astype(jnp.bfloat16)
    grad_mixed = lax.psum(contract_cols(grad_hidden, w_up).astype(jnp.bfloat16), "mp")
    right = 2 * lax.all_to_all(mixed, "dp", split_axis=1, concat_axis=0, tiled=True)
    factor = contract_cols(grad_mixed, rot_rows).astype(jnp.bfloat16)
    factor_all = lax.all_gather(factor, "dp", axis=0, tiled=True)
    spread_rows = jnp.concatenate((factor_all, acts_all), axis=0)
    skew_rows = jnp.concatenate((acts_all, -factor_all), axis=0)
    own = jnp.concatenate((acts, -factor), axis=0)
    left = lax.psum(
        (jnp.dot(factor_all, rot_half, preferred_element_type=jnp.float32) * (2 * inv_root)).astype(
            jnp.bfloat16
        ),
        "mp",
    )
    gram = lax.psum(contract_cols(spread_rows, own).astype(jnp.bfloat16), "mp")
    second = contract_rows(skew_rows, gram).astype(jnp.bfloat16)
    eye = jnp.eye(rows, dtype=jnp.float32)
    act_sq = lax.dynamic_slice(gram, (tokens + me * rows, 0), (rows, rows))
    factor_sq = lax.dynamic_slice(gram, (me * rows, rows), (rows, rows))
    squares = jnp.concatenate(
        (jnp.sum(act_sq * eye, axis=0), jnp.sum(factor_sq * -eye, axis=0))
    ).astype(jnp.bfloat16)
    packed = jnp.concatenate((second, jnp.broadcast_to(squares, (16, 2 * rows))), axis=0)
    gathered = lax.all_gather(packed, "dp", axis=0)
    width = second.shape[0]
    parts = gathered[:, width].astype(jnp.float32)
    act_norm = jnp.sum(parts[:, :rows])
    factor_norm = jnp.sum(parts[:, rows:])
    second_all = (
        gathered[:, :width].reshape(-1, width, 2, rows).transpose(1, 2, 0, 3).reshape(width, -1)
    )
    spread = (tokens ** (-0.5) + D ** (-0.5)) ** 2
    step_size = (
        step_gain
        * math.sqrt(D)
        / (jnp.sqrt((act_norm + epsilon) * (factor_norm + epsilon)) * spread)
    )
    first_map = skew_rows.T
    second_map = (
        first_map.astype(jnp.float32) - (step_size * inv_root) * second_all.astype(jnp.float32)
    ).astype(jnp.bfloat16)
    sides = jnp.concatenate((left, right), axis=0)
    half = rotation - step_size * jnp.dot(first_map, sides, preferred_element_type=jnp.float32)
    full = rotation - step_size * jnp.dot(second_map, sides, preferred_element_type=jnp.float32)
    return half, full


def solution(mesh):
    placed = (P("dp", "mp"), P(None, "mp"), P("dp", "mp"), P("mp", "dp"))
    return jax.shard_map(
        local,
        mesh=mesh,
        in_specs=placed,
        out_specs=(P("mp", "dp"), P("mp", "dp")),
        check_vma=False,
    )
```

time: 587 us -> 499 us (0.85)
  waiting for transfers between devices: 428 us -> 373 us
  matrix products: 88.4 us -> 50.4 us
  other arithmetic: 19.1 us -> 8.69 us
  blocking collectives: 32.2 us -> 40.4 us
  local copies, waits for them, and re-layouts: 2.69 us -> 9.44 us
    psum x3 -> x2, waiting for transfers between devices: 259 us -> 185 us  [the longest x1 95.4 us: local(): lax.psum((jnp.dot(factor_all, rot_half, preferred_element_type=jnp.float3...]
    dot_general x8 -> x4, matrix products: 54.5 us -> 13.7 us  [the longest x1 3.89 us: local(): jnp.dot(factor_all, rot_half, preferred_element_type=jnp.float32)]
    all_to_all x0 -> x1, blocking collectives: none -> 40.4 us  [local(): lax.all_to_all(mixed, 'dp', split_axis=1, concat_axis=0, tiled=True)]
    psum x4 -> x0, blocking collectives: 32.2 us -> none  [by_axis(): return functools.reduce(lax.psum, axes, value)]
    all_gather x2 -> x4, waiting for transfers between devices: 80.2 us -> 99 us  [the longest x1 53.8 us: local(): rot_rows = lax.all_gather(rot_half, 'dp', axis=1, tiled=True)]
    reduce_sum x3 -> x2, other arithmetic: 12 us -> 1.48 us  [the longest x1 0.81 us: local(): jnp.sum(act_sq * eye, axis=0)]
    dot_general x2 -> x3, matrix products: 27.8 us -> 30.7 us  [contract_cols(): lax.dot_general(left, right, (((1,), (1,)), ((), ())), preferred_element_...]
  transfers between devices with their start and end apart: 6 -> 7, of which waited for: 6 -> 6; matrix products, arithmetic and copies ran while one was open for 1% -> 1% of each run, Pallas kernels for 0% -> 0%
where the time goes in v1:
time: 499 us; the launch traced here: 498 us
  waiting for transfers between devices  373 us (75%)
  matrix products  50.4 us (10%)
  blocking collectives  40.4 us (8%)
  between operations  15.6 us (3%)
  local copies, waits for them, and re-layouts  9.44 us (2%)
  other arithmetic  8.69 us (2%)
    psum x1, waiting for transfers between devices, local(): lax.psum((jnp.dot(factor_all, rot_half, preferred_element_type=jnp.float3...  95.4 us
    psum x1, waiting for transfers between devices, local(): lax.psum(contract_cols(grad_hidden, w_up).astype(jnp.bfloat16), 'mp')  89.6 us
    psum x1, waiting for transfers between devices, local(): lax.psum((jnp.dot(acts, rot_rows, preferred_element_type=jnp.float32) * i...  88.7 us
    all_gather x1, waiting for transfers between devices, local(): rot_rows = lax.all_gather(rot_half, 'dp', axis=1, tiled=True)  53.8 us
    all_to_all x1, blocking collectives, local(): lax.all_to_all(mixed, 'dp', split_axis=1, concat_axis=0, tiled=True)  40.4 us
    dot_general x3, matrix products, contract_cols(): lax.dot_general(left, right, (((1,), (1,)), ((), ())), preferred_element_...  30.7 us
    all_gather x1, waiting for transfers between devices, local(): factor_all = lax.all_gather(factor, 'dp', axis=0, tiled=True)  24 us
    all_gather x1, waiting for transfers between devices, local(): acts_all = lax.all_gather(acts, 'dp', axis=0, tiled=True)  21.2 us
  transfers between devices with their start and end apart: 7, of which 6 were waited for; matrix products, arithmetic and copies ran while one was open for 1% of the time, Pallas kernels for 0%

profile of v1, /device:TPU:1, one launch (start us, length us, event | category | flops | bytes accessed | tf_op | source)
XLA Modules:
  0.0 498.1 jit_solution(1898718325875340273)
XLA Ops:
  7.2 0.0 copy-start.6
  7.2 0.0 all-gather.8.cloned.1.call-start
  7.2 2.8 convert_element_type.59
  10.0 0.0 all-gather.8.cloned.1.call-update
  10.0 0.0 all-reduce.5.cloned.1.call-start
  10.1 53.8 %all-gather.8.cloned.1.call-done = bf16[512,8192]{1,0:T(8,128)(2,1)} async-done(((bf16[512,1024]{1,0:T(8,128)(2,1)}), bf16[512,8192]{1,0:T(8,128)(2,1)}) %all-gather.8.cloned.1.call-update) | async-done | bytes 8388624 | tf_op jit(solution)/shard_map/all_gather | solution.py:31
  63.8 6.0 %fusion = bf16[128,8192]{1,0:T(8,128)(2,1)} fusion(bf16[128,512]{1,0:T(8,128)(2,1)S(1)} %copy-done.6, bf16[512,8192]{1,0:T(8,128)(2,1)} %all-gather.8.cloned.1.call-done), kind=kOutput, calls=%fused_computation.1 | convolution fusion | flops 1075838976 | bytes 10616832 | tf_op jit(solution)/shard_map/dot_general | solution.py:34
  69.9 0.0 all-reduce.5.cloned.1.call-update
  69.9 0.0 all-reduce.7.cloned.1.call-start
  69.9 88.7 %all-reduce.5.cloned.1.call-done = bf16[128,8192]{1,0:T(8,128)(2,1)} async-done(((bf16[128,8192]{1,0:T(8,128)(2,1)}), bf16[128,8192]{1,0:T(8,128)(2,1)}) %all-reduce.5.cloned.1.call-update) | async-done | bytes 2097168 | tf_op jit(solution)/shard_map/psum | solution.py:33
  158.7 20.2 %convolution_convert_fusion = bf16[128,8192]{1,0:T(8,128)(2,1)} fusion(bf16[8192,896]{1,0:T(8,128)(2,1)} %param.5, bf16[128,896]{1,0:T(8,128)(2,1)S(1)} %copy-done.8, bf16[128,8192]{1,0:T(8,128)(2,1)} %all-reduce.5.cloned.1.call-done), kind=kOutput, calls=%fused_computation.2 | convolution fusion | flops 3760291840 | bytes 19103744 | tf_op jit(solution)/shard_map/dot_general | solution.py:14
  178.9 0.0 all-reduce.7.cloned.1.call-update
  178.9 0.0 all-gather.10.cloned.1.call-start
  178.9 89.6 %all-reduce.7.cloned.1.call-done = bf16[128,8192]{1,0:T(8,128)(2,1)} async-done(((bf16[128,8192]{1,0:T(8,128)(2,1)}), bf16[128,8192]{1,0:T(8,128)(2,1)}) %all-reduce.7.cloned.1.call-update) | async-done | bytes 2097168 | tf_op jit(solution)/shard_map/psum | solution.py:44
  268.5 7.6 %fusion.16 = (bf16[128,512]{1,0:T(8,128)(2,1)S(1)}, bf16[128,512]{1,0:T(8,128)(2,1)}) fusion(bf16[128,8192]{1,0:T(8,128)(2,1)} %all-reduce.7.cloned.1.call-done, bf16[512,8192]{1,0:T(8,128)(2,1)} %all-gather.8.cloned.1.call-done), kind=kOutput, calls=%fused_computation.40 | convolution fusion | flops 1073872896 | bytes 10747904 | tf_op jit(solution)/shard_map/dot_general | solution.py:14
  276.1 0.0 all-gather.10.cloned.1.call-update
  276.1 0.0 all-gather.6.cloned.1.call-start
  276.2 0.5 all-gather.6.cloned.1.call-update
  276.7 0.0 copy-start.7
  276.7 0.0 all-reduce.9.cloned.1.call-start
  276.8 24.0 %all-gather.10.cloned.1.call-done = bf16[1024,512]{1,0:T(8,128)(2,1)} async-done(((bf16[128,512]{1,0:T(8,128)(2,1)}), bf16[1024,512]{1,0:T(8,128)(2,1)}) %all-gather.10.cloned.1.call-update) | async-done | bytes 1048592 | tf_op jit(solution)/shard_map/all_gather | solution.py:47
  300.8 3.9 multiply_convert_fusion
  304.7 21.2 %all-gather.6.cloned.1.call-done = bf16[1024,512]{1,0:T(8,128)(2,1)} async-done(((bf16[128,512]{1,0:T(8,128)(2,1)}), bf16[1024,512]{1,0:T(8,128)(2,1)}) %all-gather.6.cloned.1.call-update) | async-done | bytes 1048592 | tf_op jit(solution)/shard_map/all_gather | solution.py:32
  325.9 2.9 convolution_convert_fusion.1
  328.8 0.0 all-reduce.9.cloned.1.call-update
  328.8 0.0 all-gather.12.cloned.1.call-start
  328.9 0.2 neg.13
  329.1 95.4 %all-reduce.9.cloned.1.call-done = (bf16[1024,1024]{1,0:T(8,128)(2,1)}, bf16[2048,256]{1,0:T(8,128)(2,1)}) async-done(((bf16[1024,1024]{1,0:T(8,128)(2,1)}, bf16[2048,256]{1,0:T(8,128)(2,1)}), (bf16[1024,1024]{1,0:T(8,128)(2,1)}, bf16[2048,256]{1,0:T(8,128)(2,1)})) %all-reduce.9.cloned.1.call-update) | async-done | bytes 3145744 | tf_op jit(solution)/shard_map/psum | solution.py:51
  424.4 0.8 select_reduce_fusion
  425.3 2.4 convolution_convert_fusion.2
  427.7 0.7 pad_maximum_fusion.10
  428.5 0.0 all-gather.12.cloned.1.call-update
  428.5 0.2 copy.18
  428.7 40.4 %all_to_all.13 = bf16[128,8,1024]{2,0,1:T(8,128)(2,1)S(1)} all-to-all(bf16[128,8,1024]{2,0,1:T(8,128)(2,1)S(1)} %bitcast.33), channel_id=1, replica_groups=mesh['dp'=8,'mp'=16] {'dp'}, dimensions={1} | all-to-all | bytes 4194304 | tf_op jit(solution)/shard_map/all_to_all | solution.py:45
  469.1 1.5 broadcast_multiply_fusion
  470.5 3.0 slice.19
  473.6 0.8 slice_convert_fusion
  474.4 2.9 copy.14
  477.2 0.7 slice_reduce_fusion
  479.3 0.6 convert_multiply_fusion
  479.8 0.4 copy.12
  480.3 0.8 copy-done.5
  481.1 0.7 fusion.1
  481.8 0.8 copy-done.2
  482.7 0.6 copy-done.3
  483.3 0.6 copy-done.9
  483.9 3.7 multiply_subtract_fusion
  487.6 3.7 multiply_subtract_fusion.1
  (18 shorter events, 0.0 us)
Async XLA Ops:
  7.2 56.7 %copy-start.6 = (bf16[128,512]{1,0:T(8,128)(2,1)S(1)}, bf16[128,512]{1,0:T(8,128)(2,1)}, u32[]{:S(2)}) copy-start(bf16[128,512]{1,0:T(8,128)(2,1)} %param.4) | copy-start | bytes 393220
  7.2 56.7 %all-gather.8.cloned.1.call-start = ((), (), s32[]{:S(2)}) async-start(), calls=%async_computation.2 | async-start | bytes 9437184 | tf_op jit(solution)/shard_map/all_gather | solution.py:31
  10.0 148.6 %all-reduce.5.cloned.1.call-start = ((), (), s32[]{:S(2)}) async-start(), calls=%async_computation.3 | async-start | bytes 4194304 | tf_op jit(solution)/shard_map/psum | solution.py:33
  69.9 88.8 %copy-start.8 = (bf16[128,896]{1,0:T(8,128)(2,1)S(1)}, bf16[128,896]{1,0:T(8,128)(2,1)}, u32[]{:S(2)}) copy-start(bf16[128,896]{1,0:T(8,128)(2,1)} %param.6) | copy-start | bytes 688132
  69.9 198.6 %all-reduce.7.cloned.1.call-start = ((), (), s32[]{:S(2)}) async-start(), calls=%async_computation.4 | async-start | bytes 4194304 | tf_op jit(solution)/shard_map/psum | solution.py:44
  178.9 121.9 %copy-start.1 = (bf16[512,1024]{1,0:T(8,128)(2,1)S(1)}, bf16[512,1024]{1,0:T(8,128)(2,1)}, u32[]{:S(2)}) copy-start(bf16[512,1024]{1,0:T(8,128)(2,1)} %convert_element_type.59) | copy-start | bytes 3145732
  178.9 121.9 %all-gather.10.cloned.1.call-start = ((), (), s32[]{:S(2)}) async-start(), calls=%async_computation.5 | async-start | bytes 1179648 | tf_op jit(solution)/shard_map/all_gather | solution.py:47
  276.1 49.7 %all-gather.6.cloned.1.call-start = ((), (), s32[]{:S(2)}) async-start(), calls=%async_computation.1 | async-start | bytes 1179648 | tf_op jit(solution)/shard_map/all_gather | solution.py:32
  276.7 49.1 %copy-start.7 = (bf16[128,512]{1,0:T(8,128)(2,1)S(1)}, bf16[128,512]{1,0:T(8,128)(2,1)}, u32[]{:S(2)}) copy-start(bf16[128,512]{1,0:T(8,128)(2,1)} %param.4) | copy-start | bytes 393220
  276.7 147.7 %all-reduce.9.cloned.1.call-start = ((), (), s32[]{:S(2)}) async-start(), calls=%async_computation.7 | async-start | bytes 6291456 | tf_op jit(solution)/shard_map/psum | solution.py:51
  300.8 25.1 %copy-start.4 = (bf16[1024,512]{1,0:T(8,128)(2,1)S(1)}, bf16[1024,512]{1,0:T(8,128)(2,1)}, u32[]{:S(2)}) copy-start(bf16[1024,512]{1,0:T(8,128)(2,1)} %all-gather.10.cloned.1.call-done) | copy-start | bytes 3145732
  328.8 141.7 %all-gather.12.cloned.1.call-start = ((), (), s32[]{:S(2)}) async-start(), calls=%async_computation.6 | async-start | bytes 2433024 | tf_op jit(solution)/shard_map/all_gather | solution.py:66
  425.3 3.2 copy-start
  479.8 1.2 copy-start.5
  481.1 1.6 copy-start.2
  481.1 2.2 copy-start.3
  481.1 2.9 copy-start.9
Sparse Core Ops, SparseCore 0:
  10.3 53.5 all-gather.7
  70.0 88.5 all-reduce.4
  179.0 89.4 all-reduce.6
  276.3 24.4 all-gather.9
  302.4 23.4 all-gather.5
  329.7 94.6 all-reduce.8
  428.6 40.9 all-gather.11

commit v2 on v1

--- a/solution.py
+++ b/solution.py
@@ -1,13 +1,218 @@
+import functools
 import math
 
 import jax
 import jax.numpy as jnp
 from jax import lax
+from jax.experimental import pallas as pl
+from jax.experimental.pallas import tpu as pltpu
 from jax.sharding import PartitionSpec as P
 
 D = 8192
 step_gain = 0.5
 epsilon = 1e-06
+
+
+MESH = pl.DeviceIdType.MESH
+N_DP = 8
+SIDE = 4
+
+
+def cut(ref, dim, start, size, lead=()):
+    if dim == 1:
+        return ref.at[(*lead, slice(None), pl.ds(start, size))]
+    return ref.at[(*lead, pl.ds(start, size), slice(None))]
+
+
+def kernel(dims, modes, *refs):
+    n, e = len(dims), len(modes)
+    xs, ys = refs[:n], refs[n : n + e]
+    sums, outs = refs[n + e : 2 * n + e], refs[2 * n + e : 2 * (n + e)]
+    scratch = refs[2 * (n + e) :]
+    first, held, second = scratch[:n], scratch[n : 2 * n], scratch[2 * n : 3 * n]
+    send, recv, dp_send, dp_recv, local_sem = scratch[3 * n :]
+    dp, mp = lax.axis_index("dp"), lax.axis_index("mp")
+    at = (mp // SIDE, mp % SIDE)
+
+    def peer(axis, k):
+        j = (at[axis] + k) % SIDE
+        return j, (dp, j * SIDE + at[1] if axis == 0 else at[0] * SIDE + j)
+
+    barrier = pltpu.get_barrier_semaphore()
+    greeted = 0
+    if n:
+        for axis in (0, 1):
+            for k in range(1, SIDE):
+                pl.semaphore_signal(barrier, inc=1, device_id=peer(axis, k)[1], device_id_type=MESH)
+                greeted += 1
+    if e:
+        for k in range(1, N_DP):
+            pl.semaphore_signal(
+                barrier, inc=1, device_id=((dp + k) % N_DP, mp), device_id_type=MESH
+            )
+            greeted += 1
+    pl.semaphore_wait(barrier, greeted)
+
+    started = []
+
+    def send_to(src, dst, index, device):
+        copy = pltpu.make_async_remote_copy(
+            src_ref=src,
+            dst_ref=dst,
+            send_sem=send.at[index],
+            recv_sem=recv.at[index],
+            device_id=device,
+            device_id_type=MESH,
+        )
+        copy.start()
+        started.append(copy)
+        return copy
+
+    todo = [(h, a) for h in range(2) for a in range(n)]
+    flight = {}
+
+    def spot(a, h):
+        size = xs[a].shape[dims[a]]
+        p, q = (1, 0) if h == 0 else (0, 1)
+        return p, q, h * (size // 2), size // 8, size // 32
+
+    def index(stage, h, a, k):
+        return ((stage * 2 + h) * n + a) * 3 + k - 1
+
+    order = (2, 1, 3)
+    for h, a in todo:
+        p, q, base, big, small = spot(a, h)
+        copies = []
+        for k in order:
+            j, device = peer(p, k)
+            start = pl.multiple_of(base + j * big, big)
+            copies.append(
+                send_to(
+                    cut(xs[a], dims[a], start, big),
+                    first[a].at[h, k - 1],
+                    index(0, h, a, k),
+                    device,
+                )
+            )
+        flight[0, h, a] = copies
+    exchanges = []
+    for i, mode in enumerate(modes):
+        rows = ys[i].shape[0]
+        here = pl.multiple_of(dp * rows, rows)
+        width = outs[i].shape[1]
+
+        def part(to):
+            if mode == "gather":
+                return ys[i]
+            return ys[i].at[:, pl.ds(pl.multiple_of(to * width, width), width)]
+
+        own = pltpu.make_async_copy(part(dp), outs[i].at[pl.ds(here, rows), :], local_sem.at[i])
+        own.start()
+        exchanges.append(own)
+        for k in (4, 3, 5, 2, 6, 1, 7):
+            to = (dp + k) % N_DP
+            copy = pltpu.make_async_remote_copy(
+                src_ref=part(to),
+                dst_ref=outs[i].at[pl.ds(here, rows), :],
+                send_sem=dp_send.at[i * 7 + k - 1],
+                recv_sem=dp_recv.at[i * 7 + k - 1],
+                device_id=(to, mp),
+                device_id_type=MESH,
+            )
+            copy.start()
+            exchanges.append(copy)
+    for h, a in todo:
+        p, q, base, big, small = spot(a, h)
+        for copy in flight[0, h, a]:
+            copy.wait_recv()
+        start = pl.multiple_of(base + at[p] * big, big)
+        total = cut(xs[a], dims[a], start, big)[...].astype(jnp.float32)
+        for k in range(3):
+            total += first[a][h, k].astype(jnp.float32)
+        held[a][h] = total.astype(jnp.bfloat16)
+        copies = []
+        for k in order:
+            j, device = peer(q, k)
+            copies.append(
+                send_to(
+                    cut(held[a], dims[a], pl.multiple_of(j * small, small), small, (h,)),
+                    second[a].at[h, k - 1],
+                    index(1, h, a, k),
+                    device,
+                )
+            )
+        flight[1, h, a] = copies
+    for h, a in todo:
+        p, q, base, big, small = spot(a, h)
+        for copy in flight[1, h, a]:
+            copy.wait_recv()
+        total = cut(held[a], dims[a], pl.multiple_of(at[q] * small, small), small, (h,))[
+            ...
+        ].astype(jnp.float32)
+        for k in range(3):
+            total += second[a][h, k].astype(jnp.float32)
+        block = cut(
+            sums[a], dims[a], pl.multiple_of(base + at[p] * big + at[q] * small, small), small
+        )
+        block[...] = total.astype(jnp.bfloat16)
+        flight[2, h, a] = [
+            send_to(block, block, index(2, h, a, k), peer(q, k)[1]) for k in order
+        ]
+    for h, a in todo:
+        p, q, base, big, small = spot(a, h)
+        for copy in flight[2, h, a]:
+            copy.wait_recv()
+        block = cut(sums[a], dims[a], pl.multiple_of(base + at[p] * big, big), big)
+        flight[3, h, a] = [
+            send_to(block, block, index(3, h, a, k), peer(p, k)[1]) for k in order
+        ]
+    for h, a in todo:
+        for copy in flight[3, h, a]:
+            copy.wait_recv()
+    for copy in started:
+        copy.wait_send()
+    for copy in exchanges:
+        copy.wait()
+
+
+def communicate(number, name, adds=(), moves=()):
+    dims = [dim for _, dim in adds]
+    modes = [mode for _, mode in moves]
+    arrays = [x for x, _ in adds] + [y for y, _ in moves]
+    shapes = [x.shape for x, _ in adds]
+    for y, mode in moves:
+        width = y.shape[1] if mode == "gather" else y.shape[1] // N_DP
+        shapes.append((y.shape[0] * N_DP, width))
+
+    def piece(x, dim, parts):
+        shape = list(x.shape)
+        shape[dim] //= parts
+        return tuple(shape)
+
+    first = [pltpu.VMEM((2, 3, *piece(x, d, 8)), jnp.bfloat16) for x, d in adds]
+    held = [pltpu.VMEM((2, *piece(x, d, 8)), jnp.bfloat16) for x, d in adds]
+    second = [pltpu.VMEM((2, 3, *piece(x, d, 32)), jnp.bfloat16) for x, d in adds]
+    dma = pltpu.SemaphoreType.DMA
+    return pl.pallas_call(
+        functools.partial(kernel, dims, modes),
+        out_shape=[jax.ShapeDtypeStruct(s, jnp.bfloat16) for s in shapes],
+        in_specs=[pl.BlockSpec(memory_space=pltpu.VMEM)] * len(arrays),
+        out_specs=[pl.BlockSpec(memory_space=pltpu.VMEM)] * len(arrays),
+        scratch_shapes=[
+            *first,
+            *held,
+            *second,
+            dma((max(24 * len(adds), 1),)),
+            dma((max(24 * len(adds), 1),)),
+            dma((max(7 * len(moves), 1),)),
+            dma((max(7 * len(moves), 1),)),
+            dma((max(len(moves), 1),)),
+        ],
+        compiler_params=pltpu.CompilerParams(
+            collective_id=number, has_side_effects=True, vmem_limit_bytes=32 * 1024 * 1024
+        ),
+        name=name,
+    )(*arrays)
 
 
 def contract_cols(left, right):
@@ -29,32 +234,28 @@
     tokens = rows * lax.axis_size("dp")
     rot_half = rotation.astype(jnp.bfloat16)
     rot_rows = lax.all_gather(rot_half, "dp", axis=1, tiled=True)
-    acts_all = lax.all_gather(acts, "dp", axis=0, tiled=True)
-    mixed = lax.psum(
-        (jnp.dot(acts, rot_rows, preferred_element_type=jnp.float32) * inv_root).astype(
-            jnp.bfloat16
-        ),
-        "mp",
-    )
+    mixed_part = (jnp.dot(acts, rot_rows, preferred_element_type=jnp.float32) * inv_root).astype(
+        jnp.bfloat16
+    )
+    mixed, acts_all = communicate(0, "sum_mixed", [(mixed_part, 1)], [(acts, "gather")])
     hidden = jnp.dot(mixed, w_up, preferred_element_type=jnp.float32)
     sigmoid_hidden = jax.nn.sigmoid(hidden)
     grad_hidden = (
         out_grad.astype(jnp.float32) * sigmoid_hidden * (1.0 + hidden * (1.0 - sigmoid_hidden))
     ).astype(jnp.bfloat16)
-    grad_mixed = lax.psum(contract_cols(grad_hidden, w_up).astype(jnp.bfloat16), "mp")
-    right = 2 * lax.all_to_all(mixed, "dp", split_axis=1, concat_axis=0, tiled=True)
+    grad_part = contract_cols(grad_hidden, w_up).astype(jnp.bfloat16)
+    grad_mixed, right = communicate(1, "sum_grad", [(grad_part, 1)], [(mixed, "transpose")])
+    right = 2 * right
     factor = contract_cols(grad_mixed, rot_rows).astype(jnp.bfloat16)
-    factor_all = lax.all_gather(factor, "dp", axis=0, tiled=True)
+    (factor_all,) = communicate(2, "gather_factor", [], [(factor, "gather")])
     spread_rows = jnp.concatenate((factor_all, acts_all), axis=0)
     skew_rows = jnp.concatenate((acts_all, -factor_all), axis=0)
     own = jnp.concatenate((acts, -factor), axis=0)
-    left = lax.psum(
-        (jnp.dot(factor_all, rot_half, preferred_element_type=jnp.float32) * (2 * inv_root)).astype(
-            jnp.bfloat16
-        ),
-        "mp",
-    )
-    gram = lax.psum(contract_cols(spread_rows, own).astype(jnp.bfloat16), "mp")
+    left_part = (
+        jnp.dot(factor_all, rot_half, preferred_element_type=jnp.float32) * (2 * inv_root)
+    ).astype(jnp.bfloat16)
+    gram_part = contract_cols(spread_rows, own).astype(jnp.bfloat16)
+    (gram,) = communicate(3, "sum_gram", [(gram_part, 0)], [])
     second = contract_rows(skew_rows, gram).astype(jnp.bfloat16)
     eye = jnp.eye(rows, dtype=jnp.float32)
     act_sq = lax.dynamic_slice(gram, (tokens + me * rows, 0), (rows, rows))
@@ -63,7 +264,8 @@
         (jnp.sum(act_sq * eye, axis=0), jnp.sum(factor_sq * -eye, axis=0))
     ).astype(jnp.bfloat16)
     packed = jnp.concatenate((second, jnp.broadcast_to(squares, (16, 2 * rows))), axis=0)
-    gathered = lax.all_gather(packed, "dp", axis=0)
+    left, gathered = communicate(4, "sum_left", [(left_part, 0)], [(packed, "gather")])
+    gathered = gathered.reshape(-1, *packed.shape)
     width = second.shape[0]
     parts = gathered[:, width].astype(jnp.float32)
     act_norm = jnp.sum(parts[:, :rows])

time: 499 us -> 302 us (0.61)
  waiting for transfers between devices: 373 us -> 53.9 us
  Pallas kernels: 0 us -> 163 us
  blocking collectives: 40.4 us -> 0 us
  local copies, waits for them, and re-layouts: 9.44 us -> 19.4 us
  matrix products: 50.4 us -> 41 us
    psum x3 -> x0, waiting for transfers between devices: 274 us -> none  [the longest x1 95.4 us: local(): lax.psum((jnp.dot(factor_all, rot_half, preferred_element_type=jnp.float3...]
    pallas_call x0 -> x5, Pallas kernels: none -> 163 us  [communicate(): pl.pallas_call(functools.partial(kernel, dims, modes), out_shape=[jax.Sha...]
    all_gather x3 -> x0, waiting for transfers between devices: 45.2 us -> none  [the longest x1 24 us: local(): factor_all = lax.all_gather(factor, 'dp', axis=0, tiled=True)]
    all_to_all x1 -> x0, blocking collectives: 40.4 us -> none  [local(): lax.all_to_all(mixed, 'dp', split_axis=1, concat_axis=0, tiled=True)]
    mul x1 -> x2, local copies, waits for them, and re-layouts: 0.44 us -> 13.1 us  [local(): step_size * inv_root * second_all.astype(jnp.float32)]
  transfers between devices with their start and end apart: 7 -> 1, of which waited for: 6 -> 1; matrix products, arithmetic and copies ran while one was open for 1% -> 0% of each run, Pallas kernels for 0% -> 0%
where the time goes in v2:
time: 302 us
  Pallas kernels  163 us (54%)
  waiting for transfers between devices  53.9 us (18%)
  matrix products  41 us (14%)
  local copies, waits for them, and re-layouts  19.4 us (6%)
  between operations  15.7 us (5%)
  other arithmetic  9.25 us (3%)
    pallas_call x5, Pallas kernels, communicate(): pl.pallas_call(functools.partial(kernel, dims, modes), out_shape=[jax.Sha...  163 us
    all_gather x1, waiting for transfers between devices, local(): rot_rows = lax.all_gather(rot_half, 'dp', axis=1, tiled=True)  53.8 us
    dot_general x3, matrix products, contract_cols(): lax.dot_general(left, right, (((1,), (1,)), ((), ())), preferred_element_...  26.9 us
    mul x2, local copies, waits for them, and re-layouts, local(): step_size * inv_root * second_all.astype(jnp.float32)  13.1 us
    unnamed x23, local copies, waits for them, and re-layouts  6.32 us
  transfers between devices with their start and end apart: 1, of which 1 were waited for; matrix products, arithmetic and copies ran while one was open for 0% of the time, Pallas kernels for 0%

profile of v2, /device:TPU:1, one launch (start us, length us, event | category | flops | bytes accessed | tf_op | source)
XLA Modules:
  0.0 301.9 jit_solution(9831643782024885221)
XLA Ops:
  7.2 0.0 copy-start.3
  7.2 0.0 all-gather.2.cloned.1.call-start
  7.2 2.8 convert_element_type.59
  10.0 0.0 all-gather.2.cloned.1.call-update
  10.0 53.8 %all-gather.2.cloned.1.call-done = bf16[512,8192]{1,0:T(8,128)(2,1)} async-done(((bf16[512,1024]{1,0:T(8,128)(2,1)}), bf16[512,8192]{1,0:T(8,128)(2,1)}) %all-gather.2.cloned.1.call-update) | async-done | bytes 8388624 | tf_op jit(solution)/shard_map/all_gather | solution.py:236
  63.8 0.0 copy-done.3
  63.8 4.7 %fusion.refs_0_ = bf16[128,8192]{1,0:T(8,128)(2,1)S(1)} fusion(bf16[128,512]{1,0:T(8,128)(2,1)S(1)} %copy-done.3, bf16[512,8192]{1,0:T(8,128)(2,1)} %all-gather.2.cloned.1.call-done), kind=kOutput, calls=%fused_computation.1 | convolution fusion | flops 1075838976 | bytes 10616832 | tf_op jit(solution)/shard_map/dot_general | solution.py:237
  68.5 0.0 copy-start.10
  68.5 41.3 %sum_mixed.1 = (bf16[128,8192]{1,0:T(8,128)(2,1)S(1)}, bf16[1024,512]{1,0:T(8,128)(2,1)S(1)}) custom-call(bf16[128,8192]{1,0:T(8,128)(2,1)S(1)} %fusion.refs_0_, bf16[128,512]{1,0:T(8,128)(2,1)S(1)} %copy-done.3), custom_call_target="tpu_custom_call" | custom-call | tf_op jit(solution)/shard_map/sum_mixed/pallas_call | solution.py:196
  109.9 0.0 copy-done.10
  109.9 19.8 %convolution_convert_fusion.refs_0_ = bf16[128,8192]{1,0:T(8,128)(2,1)} fusion(bf16[8192,896]{1,0:T(8,128)(2,1)} %param.5, bf16[128,896]{1,0:T(8,128)(2,1)S(1)} %copy-done.10, bf16[128,8192]{1,0:T(8,128)(2,1)S(1)} %get-tuple-element.8.refs_1_), kind=kOutput, calls=%fused_computation.2 | convolution fusion | flops 3760291840 | bytes 19103744 | tf_op jit(solution)/shard_map/dot_general | solution.py:219
  129.6 0.0 copy-start
  129.7 1.6 copy-done
  131.2 39.2 %sum_grad.1 = (bf16[128,8192]{1,0:T(8,128)(2,1)S(1)}, bf16[1024,1024]{1,0:T(8,128)(2,1)S(1)}) custom-call(bf16[128,8192]{1,0:T(8,128)(2,1)S(1)} %copy-done, bf16[128,8192]{1,0:T(8,128)(2,1)S(1)} %get-tuple-element.8.refs_1_), custom_call_target="tpu_custom_call" | custom-call | tf_op jit(solution)/shard_map/sum_grad/pallas_call | solution.py:196
  170.5 0.0 copy-start.1
  170.5 1.3 copy-done.1
  171.8 6.4 %fusion.16 = (bf16[128,512]{1,0:T(8,128)(2,1)S(1)}, bf16[128,512]{1,0:T(8,128)(2,1)S(1)}) fusion(bf16[128,8192]{1,0:T(8,128)(2,1)S(1)} %get-tuple-element.9, bf16[512,8192]{1,0:T(8,128)(2,1)} %all-gather.2.cloned.1.call-done), kind=kOutput, calls=%fused_computation.39 | convolution fusion | flops 1073872896 | bytes 10747904 | tf_op jit(solution)/shard_map/dot_general | solution.py:219
  178.2 0.0 copy-start.6
  178.2 15.8 %gather_factor.1 = bf16[1024,512]{1,0:T(8,128)(2,1)S(1)} custom-call(bf16[128,512]{1,0:T(8,128)(2,1)S(1)} %get-tuple-element.19.refs_0_), custom_call_target="tpu_custom_call" | custom-call | tf_op jit(solution)/shard_map/gather_factor/pallas_call | solution.py:196
  194.1 0.2 neg.13
  194.3 0.0 copy-done.6
  194.3 0.0 copy-start.7
  194.3 1.3 multiply_convert_fusion.refs_0_
  195.5 0.7 convolution_convert_fusion.1.refs_0_
  196.3 22.7 %sum_gram.1 = bf16[2048,256]{1,0:T(8,128)(2,1)S(1)} custom-call(bf16[2048,256]{1,0:T(8,128)(2,1)S(1)} %convolution_convert_fusion.1.refs_0_), custom_call_target="tpu_custom_call" | custom-call | tf_op jit(solution)/shard_map/sum_gram/pallas_call | solution.py:196
  218.9 0.0 copy-done.7
  218.9 0.8 convolution_convert_fusion.2
  219.8 43.7 %sum_left.1 = (bf16[1024,1024]{1,0:T(8,128)(2,1)S(1)}, bf16[4224,256]{1,0:T(8,128)(2,1)S(1)}) custom-call(bf16[1024,1024]{1,0:T(8,128)(2,1)S(1)} %multiply_convert_fusion.refs_0_, bf16[528,256]{1,0:T(8,128)(2,1)S(1)} %pad_maximum_fusion.10.refs_1_), custom_call_target="tpu_custom_call" | custom-call | tf_op jit(solution)/shard_map/sum_left/pallas_call | solution.py:196
  263.5 0.0 copy-start.4
  263.5 1.3 copy-done.4
  264.9 0.7 slice_reduce_fusion
  266.9 2.4 convert_multiply_fusion
  269.3 5.8 %mul.90 = f32[8,512,2,128]{3,2,1,0:T(2,128)} reshape(f32[8,512,256]{2,1,0:T(8,128)} %convert_multiply_fusion) | data formatting | bytes 8388608 | tf_op jit(solution)/shard_map/mul | solution.py:284
  275.0 0.0 copy-start.8
  275.0 7.3 %copy.6 = f32[8,512,2,128]{1,3,0,2:T(8,128)} copy(f32[8,512,2,128]{3,2,1,0:T(2,128)} %mul.90) | data formatting | bytes 8388608 | tf_op jit(solution)/shard_map/mul | solution.py:284
  282.4 0.0 copy-done.8
  282.4 0.0 copy-start.2
  282.4 3.1 %fusion.1 = bf16[512,2048]{0,1:T(8,128)(2,1)S(1)} fusion(f32[8,512,2,128]{1,3,0,2:T(8,128)} %copy.6, bf16[1024,512]{1,0:T(8,128)(2,1)S(1)} %copy-done.8, bf16[1024,512]{1,0:T(8,128)(2,1)S(1)} %get-tuple-element.10), kind=kLoop, calls=%fused_computation.5 | loop fusion | flops 6291456 | bytes 8388608 | tf_op jit(solution)/shard_map/convert_element_type | solution.py:285
  285.4 0.0 copy-done.2
  285.4 0.0 copy-start.5
  285.5 0.0 copy-start.9
  285.5 0.1 broadcast_multiply_fusion
  285.6 1.4 copy-done.5
  287.0 0.6 copy-done.9
  287.7 3.7 %multiply_subtract_fusion.1 = f32[512,1024]{1,0:T(8,128)} fusion(f32[512,1024]{1,0:T(8,128)S(1)} %copy-done.9, bf16[1024,1024]{1,0:T(8,128)(2,1)S(1)} %broadcast_multiply_fusion, bf16[1024,1024]{1,0:T(8,128)(2,1)S(1)} %copy-done.5, f32[]{:T(128)S(6)} %div.7, bf16[1024,512]{1,0:T(8,128)(2,1)S(1)} %copy-done.8, bf16[1024,512]{1,0:T(8,128)(2,1)S(1)} %get-tuple-element.10), kind=kOutput, calls=%fused_computation.16 | convolution fusion | flops 2161115136 | bytes 10485764 | tf_op jit(solution)/shard_map/dot_general | solution.py:287
  291.4 3.7 %multiply_subtract_fusion = f32[512,1024]{1,0:T(8,128)} fusion(f32[512,1024]{1,0:T(8,128)S(1)} %copy-done.9, bf16[512,2048]{0,1:T(8,128)(2,1)S(1)} %fusion.1, bf16[1024,1024]{1,0:T(8,128)(2,1)S(1)} %broadcast_multiply_fusion, bf16[1024,1024]{1,0:T(8,128)(2,1)S(1)} %copy-done.5, f32[]{:T(128)S(6)} %div.7), kind=kOutput, calls=%fused_computation.15 | convolution fusion | flops 2156920832 | bytes 10485764 | tf_op jit(solution)/shard_map/dot_general | solution.py:288
  (6 shorter events, 0.1 us)
Async XLA Ops:
  7.2 56.7 %copy-start.3 = (bf16[128,512]{1,0:T(8,128)(2,1)S(1)}, bf16[128,512]{1,0:T(8,128)(2,1)}, u32[]{:S(2)}) copy-start(bf16[128,512]{1,0:T(8,128)(2,1)} %refs_1_.1) | copy-start | bytes 393220
  7.2 56.7 %all-gather.2.cloned.1.call-start = ((), (), s32[]{:S(2)}) async-start(), calls=%async_computation | async-start | bytes 9437184 | tf_op jit(solution)/shard_map/all_gather | solution.py:236
  68.5 41.3 %copy-start.10 = (bf16[128,896]{1,0:T(8,128)(2,1)S(1)}, bf16[128,896]{1,0:T(8,128)(2,1)}, u32[]{:S(2)}) copy-start(bf16[128,896]{1,0:T(8,128)(2,1)} %param.6) | copy-start | bytes 688132
  129.6 1.6 copy-start
  170.5 1.3 copy-start.1
  178.2 16.0 %copy-start.6 = (bf16[512,1024]{1,0:T(8,128)(2,1)S(1)}, bf16[512,1024]{1,0:T(8,128)(2,1)}, u32[]{:S(2)}) copy-start(bf16[512,1024]{1,0:T(8,128)(2,1)} %convert_element_type.59) | copy-start | bytes 3145732
  194.3 24.7 %copy-start.7 = (bf16[1024,512]{1,0:T(8,128)(2,1)}, bf16[1024,512]{1,0:T(8,128)(2,1)S(1)}, u32[]{:S(2)}) copy-start(bf16[1024,512]{1,0:T(8,128)(2,1)S(1)} %neg.13) | copy-start | bytes 3145732
  263.5 1.3 copy-start.4
  275.0 7.3 %copy-start.8 = (bf16[1024,512]{1,0:T(8,128)(2,1)S(1)}, bf16[1024,512]{1,0:T(8,128)(2,1)}, u32[]{:S(2)}) copy-start(bf16[1024,512]{1,0:T(8,128)(2,1)} %copy-done.7) | copy-start | bytes 3145732
  282.4 3.1 %copy-start.2 = (bf16[1024,1024]{1,0:T(8,128)(2,1)S(1)}, bf16[1024,1024]{1,0:T(8,128)(2,1)}, u32[]{:S(2)}) copy-start(bf16[1024,1024]{1,0:T(8,128)(2,1)} %copy-done.1) | copy-start | bytes 6291460
  285.4 1.6 copy-start.5
  285.5 2.2 copy-start.9
Sparse Core Ops, SparseCore 0:
  10.3 53.5 all-gather.1

commit v3 on v2

--- a/solution.py
+++ b/solution.py
@@ -24,8 +24,8 @@
     return ref.at[(*lead, pl.ds(start, size), slice(None))]
 
 
-def kernel(dims, modes, *refs):
-    n, e = len(dims), len(modes)
+def kernel(dims, arrays, modes, *refs):
+    n, e = len(dims), arrays
     xs, ys = refs[:n], refs[n : n + e]
     sums, outs = refs[n + e : 2 * n + e], refs[2 * n + e : 2 * (n + e)]
     scratch = refs[2 * (n + e) :]
@@ -97,23 +97,25 @@
         flight[0, h, a] = copies
     exchanges = []
     for i, mode in enumerate(modes):
-        rows = ys[i].shape[0]
-        here = pl.multiple_of(dp * rows, rows)
-        width = outs[i].shape[1]
+        which, block, blocks, split = mode
+        rows = ys[which].shape[0] // blocks
+        here = pl.ds(pl.multiple_of((block * N_DP + dp) * rows, rows), rows)
+        width = outs[which].shape[1]
 
         def part(to):
-            if mode == "gather":
-                return ys[i]
-            return ys[i].at[:, pl.ds(pl.multiple_of(to * width, width), width)]
-
-        own = pltpu.make_async_copy(part(dp), outs[i].at[pl.ds(here, rows), :], local_sem.at[i])
+            if not split:
+                return ys[which].at[pl.ds(block * rows, rows), :]
+            return ys[which].at[:, pl.ds(pl.multiple_of(to * width, width), width)]
+
+        landing = outs[which].at[here, :]
+        own = pltpu.make_async_copy(part(dp), landing, local_sem.at[i])
         own.start()
         exchanges.append(own)
         for k in (4, 3, 5, 2, 6, 1, 7):
             to = (dp + k) % N_DP
             copy = pltpu.make_async_remote_copy(
                 src_ref=part(to),
-                dst_ref=outs[i].at[pl.ds(here, rows), :],
+                dst_ref=landing,
                 send_sem=dp_send.at[i * 7 + k - 1],
                 recv_sem=dp_recv.at[i * 7 + k - 1],
                 device_id=(to, mp),
@@ -177,11 +179,16 @@
 
 def communicate(number, name, adds=(), moves=()):
     dims = [dim for _, dim in adds]
-    modes = [mode for _, mode in moves]
+    modes = []
+    for i, (_, mode) in enumerate(moves):
+        if mode == "transpose":
+            modes.append((i, 0, 1, True))
+        else:
+            modes.extend((i, s, mode, False) for s in range(mode))
     arrays = [x for x, _ in adds] + [y for y, _ in moves]
     shapes = [x.shape for x, _ in adds]
     for y, mode in moves:
-        width = y.shape[1] if mode == "gather" else y.shape[1] // N_DP
+        width = y.shape[1] // N_DP if mode == "transpose" else y.shape[1]
         shapes.append((y.shape[0] * N_DP, width))
 
     def piece(x, dim, parts):
@@ -194,7 +201,7 @@
     second = [pltpu.VMEM((2, 3, *piece(x, d, 32)), jnp.bfloat16) for x, d in adds]
     dma = pltpu.SemaphoreType.DMA
     return pl.pallas_call(
-        functools.partial(kernel, dims, modes),
+        functools.partial(kernel, dims, len(moves), modes),
         out_shape=[jax.ShapeDtypeStruct(s, jnp.bfloat16) for s in shapes],
         in_specs=[pl.BlockSpec(memory_space=pltpu.VMEM)] * len(arrays),
         out_specs=[pl.BlockSpec(memory_space=pltpu.VMEM)] * len(arrays),
@@ -204,9 +211,9 @@
             *second,
             dma((max(24 * len(adds), 1),)),
             dma((max(24 * len(adds), 1),)),
-            dma((max(7 * len(moves), 1),)),
-            dma((max(7 * len(moves), 1),)),
-            dma((max(len(moves), 1),)),
+            dma((max(7 * len(modes), 1),)),
+            dma((max(7 * len(modes), 1),)),
+            dma((max(len(modes), 1),)),
         ],
         compiler_params=pltpu.CompilerParams(
             collective_id=number, has_side_effects=True, vmem_limit_bytes=32 * 1024 * 1024
@@ -237,7 +244,7 @@
     mixed_part = (jnp.dot(acts, rot_rows, preferred_element_type=jnp.float32) * inv_root).astype(
         jnp.bfloat16
     )
-    mixed, acts_all = communicate(0, "sum_mixed", [(mixed_part, 1)], [(acts, "gather")])
+    mixed, acts_all = communicate(0, "sum_mixed", [(mixed_part, 1)], [(acts, 1)])
     hidden = jnp.dot(mixed, w_up, preferred_element_type=jnp.float32)
     sigmoid_hidden = jax.nn.sigmoid(hidden)
     grad_hidden = (
@@ -247,7 +254,7 @@
     grad_mixed, right = communicate(1, "sum_grad", [(grad_part, 1)], [(mixed, "transpose")])
     right = 2 * right
     factor = contract_cols(grad_mixed, rot_rows).astype(jnp.bfloat16)
-    (factor_all,) = communicate(2, "gather_factor", [], [(factor, "gather")])
+    (factor_all,) = communicate(2, "gather_factor", [], [(factor, 1)])
     spread_rows = jnp.concatenate((factor_all, acts_all), axis=0)
     skew_rows = jnp.concatenate((acts_all, -factor_all), axis=0)
     own = jnp.concatenate((acts, -factor), axis=0)
@@ -256,36 +263,32 @@
     ).astype(jnp.bfloat16)
     gram_part = contract_cols(spread_rows, own).astype(jnp.bfloat16)
     (gram,) = communicate(3, "sum_gram", [(gram_part, 0)], [])
-    second = contract_rows(skew_rows, gram).astype(jnp.bfloat16)
+    second = contract_rows(gram, skew_rows).astype(jnp.bfloat16)
     eye = jnp.eye(rows, dtype=jnp.float32)
     act_sq = lax.dynamic_slice(gram, (tokens + me * rows, 0), (rows, rows))
     factor_sq = lax.dynamic_slice(gram, (me * rows, rows), (rows, rows))
     squares = jnp.concatenate(
         (jnp.sum(act_sq * eye, axis=0), jnp.sum(factor_sq * -eye, axis=0))
     ).astype(jnp.bfloat16)
-    packed = jnp.concatenate((second, jnp.broadcast_to(squares, (16, 2 * rows))), axis=0)
-    left, gathered = communicate(4, "sum_left", [(left_part, 0)], [(packed, "gather")])
-    gathered = gathered.reshape(-1, *packed.shape)
-    width = second.shape[0]
-    parts = gathered[:, width].astype(jnp.float32)
+    squares = jnp.broadcast_to(squares, (16, 2 * rows))
+    left, second_all, parts = communicate(
+        4, "sum_left", [(left_part, 0)], [(second, 2), (squares, 1)]
+    )
+    parts = parts[::16].astype(jnp.float32)
     act_norm = jnp.sum(parts[:, :rows])
     factor_norm = jnp.sum(parts[:, rows:])
-    second_all = (
-        gathered[:, :width].reshape(-1, width, 2, rows).transpose(1, 2, 0, 3).reshape(width, -1)
-    )
     spread = (tokens ** (-0.5) + D ** (-0.5)) ** 2
     step_size = (
         step_gain
         * math.sqrt(D)
         / (jnp.sqrt((act_norm + epsilon) * (factor_norm + epsilon)) * spread)
     )
-    first_map = skew_rows.T
     second_map = (
-        first_map.astype(jnp.float32) - (step_size * inv_root) * second_all.astype(jnp.float32)
+        skew_rows.astype(jnp.float32) - (step_size * inv_root) * second_all.astype(jnp.float32)
     ).astype(jnp.bfloat16)
     sides = jnp.concatenate((left, right), axis=0)
-    half = rotation - step_size * jnp.dot(first_map, sides, preferred_element_type=jnp.float32)
-    full = rotation - step_size * jnp.dot(second_map, sides, preferred_element_type=jnp.float32)
+    half = rotation - step_size * contract_rows(skew_rows, sides)
+    full = rotation - step_size * contract_rows(second_map, sides)
     return half, full
 
 

time: 302 us -> 288 us (0.954)
  local copies, waits for them, and re-layouts: 19.4 us -> 5.62 us
  other arithmetic: 9.25 us -> 5.13 us
  matrix products: 41 us -> 44.3 us
    mul x2 -> x0, local copies, waits for them, and re-layouts: 13.1 us -> none  [local(): step_size * inv_root * second_all.astype(jnp.float32)]
    dot_general x1 -> x3, matrix products: 0.75 us -> 11.5 us  [contract_rows(): lax.dot_general(left, right, (((0,), (0,)), ((), ())), preferred_element_...]
    dot_general x2 -> x0, matrix products: 7.41 us -> none  [the longest x1 3.71 us: local(): jnp.dot(second_map, sides, preferred_element_type=jnp.float32)]
    convert_element_type x2 -> x1, other arithmetic: 3.06 us -> 0.01 us  [local(): parts = parts[::16].astype(jnp.float32)]
    unnamed x23 -> x28, local copies, waits for them, and re-layouts: 6.32 us -> 5.6 us
where the time goes in v3:
time: 288 us
  Pallas kernels  163 us (57%)
  waiting for transfers between devices  53.9 us (19%)
  matrix products  44.3 us (15%)
  between operations  15.7 us (5%)
  local copies, waits for them, and re-layouts  5.62 us (2%)
  other arithmetic  5.13 us (2%)
    pallas_call x5, Pallas kernels, communicate(): pl.pallas_call(functools.partial(kernel, dims, len(moves), modes), out_sh...  163 us
    all_gather x1, waiting for transfers between devices, local(): rot_rows = lax.all_gather(rot_half, 'dp', axis=1, tiled=True)  53.8 us
    dot_general x3, matrix products, contract_cols(): lax.dot_general(left, right, (((1,), (1,)), ((), ())), preferred_element_...  26.9 us
    dot_general x3, matrix products, contract_rows(): lax.dot_general(left, right, (((0,), (0,)), ((), ())), preferred_element_...  11.5 us
  transfers between devices with their start and end apart: 1, of which 1 were waited for; matrix products, arithmetic and copies ran while one was open for 0% of the time, Pallas kernels for 0%

profile of v3, /device:TPU:1, one launch (start us, length us, event | category | flops | bytes accessed | tf_op | source)
XLA Modules:
  0.0 287.7 jit_solution(14298501910937595978)
XLA Ops:
  7.2 0.0 copy-start.3
  7.2 0.0 all-gather.2.cloned.1.call-start
  7.2 2.8 convert_element_type.50
  10.0 0.0 all-gather.2.cloned.1.call-update
  10.0 53.8 %all-gather.2.cloned.1.call-done = bf16[512,8192]{1,0:T(8,128)(2,1)} async-done(((bf16[512,1024]{1,0:T(8,128)(2,1)}), bf16[512,8192]{1,0:T(8,128)(2,1)}) %all-gather.2.cloned.1.call-update) | async-done | bytes 8388624 | tf_op jit(solution)/shard_map/all_gather | solution.py:243
  63.8 0.0 copy-done.3
  63.8 4.7 %fusion.refs_0_ = bf16[128,8192]{1,0:T(8,128)(2,1)S(1)} fusion(bf16[128,512]{1,0:T(8,128)(2,1)S(1)} %copy-done.3, bf16[512,8192]{1,0:T(8,128)(2,1)} %all-gather.2.cloned.1.call-done), kind=kOutput, calls=%fused_computation.1 | convolution fusion | flops 1075838976 | bytes 10616832 | tf_op jit(solution)/shard_map/dot_general | solution.py:244
  68.5 0.0 copy-start.13
  68.5 41.3 %sum_mixed.1 = (bf16[128,8192]{1,0:T(8,128)(2,1)S(1)}, bf16[1024,512]{1,0:T(8,128)(2,1)S(1)}) custom-call(bf16[128,8192]{1,0:T(8,128)(2,1)S(1)} %fusion.refs_0_, bf16[128,512]{1,0:T(8,128)(2,1)S(1)} %copy-done.3), custom_call_target="tpu_custom_call" | custom-call | tf_op jit(solution)/shard_map/sum_mixed/pallas_call | solution.py:203
  109.9 0.0 copy-done.13
  109.9 19.8 %convolution_convert_fusion.refs_0_ = bf16[128,8192]{1,0:T(8,128)(2,1)} fusion(bf16[8192,896]{1,0:T(8,128)(2,1)} %param.5, bf16[128,896]{1,0:T(8,128)(2,1)S(1)} %copy-done.13, bf16[128,8192]{1,0:T(8,128)(2,1)S(1)} %get-tuple-element.9.refs_1_), kind=kOutput, calls=%fused_computation.2 | convolution fusion | flops 3760291840 | bytes 19103744 | tf_op jit(solution)/shard_map/dot_general | solution.py:226
  129.6 0.0 copy-start
  129.7 1.6 copy-done
  131.2 39.2 %sum_grad.1 = (bf16[128,8192]{1,0:T(8,128)(2,1)S(1)}, bf16[1024,1024]{1,0:T(8,128)(2,1)S(1)}) custom-call(bf16[128,8192]{1,0:T(8,128)(2,1)S(1)} %copy-done, bf16[128,8192]{1,0:T(8,128)(2,1)S(1)} %get-tuple-element.9.refs_1_), custom_call_target="tpu_custom_call" | custom-call | tf_op jit(solution)/shard_map/sum_grad/pallas_call | solution.py:203
  170.5 0.0 copy-start.1
  170.5 1.3 copy-done.1
  171.8 6.4 %fusion.16 = (bf16[128,512]{1,0:T(8,128)(2,1)S(1)}, bf16[128,512]{1,0:T(8,128)(2,1)S(1)}) fusion(bf16[128,8192]{1,0:T(8,128)(2,1)S(1)} %get-tuple-element.10, bf16[512,8192]{1,0:T(8,128)(2,1)} %all-gather.2.cloned.1.call-done), kind=kOutput, calls=%fused_computation.35 | convolution fusion | flops 1073872896 | bytes 10747904 | tf_op jit(solution)/shard_map/dot_general | solution.py:226
  178.2 0.0 copy-start.8
  178.2 15.8 %gather_factor.1 = bf16[1024,512]{1,0:T(8,128)(2,1)S(1)} custom-call(bf16[128,512]{1,0:T(8,128)(2,1)S(1)} %get-tuple-element.21.refs_0_), custom_call_target="tpu_custom_call" | custom-call | tf_op jit(solution)/shard_map/gather_factor/pallas_call | solution.py:203
  194.1 0.2 neg.14
  194.3 0.0 copy-done.8
  194.3 0.0 copy-start.11
  194.3 1.3 multiply_convert_fusion.refs_0_
  195.5 0.7 convolution_convert_fusion.1.refs_0_
  196.3 22.7 %sum_gram.1 = bf16[2048,256]{1,0:T(8,128)(2,1)S(1)} custom-call(bf16[2048,256]{1,0:T(8,128)(2,1)S(1)} %convolution_convert_fusion.1.refs_0_), custom_call_target="tpu_custom_call" | custom-call | tf_op jit(solution)/shard_map/sum_gram/pallas_call | solution.py:203
  218.9 0.0 copy-done.11
  218.9 0.7 convolution_convert_fusion.2.refs_1_
  219.7 0.0 copy-start.2
  219.8 44.0 %sum_left.1 = (bf16[1024,1024]{1,0:T(8,128)(2,1)S(1)}, bf16[2048,512]{1,0:T(8,128)(2,1)S(1)}, bf16[128,256]{1,0:T(8,128)(2,1)S(1)}) custom-call(bf16[1024,1024]{1,0:T(8,128)(2,1)S(1)} %multiply_convert_fusion.refs_0_, bf16[256,512]{1,0:T(8,128)(2,1)S(1)} %convolution_convert_fusion.2.refs_1_, bf16[16,256]{1,0:T(8,128)(2,1)S(1)} %broadcast_in_dim.3.refs_2_), custom_call_target="tpu_custom_call" | custom-call | tf_op jit(solution)/shard_map/sum_left/pallas_call | solution.py:203
  263.8 0.0 copy-start.4
  263.8 1.3 copy-done.4
  265.1 0.0 copy-start.6
  265.1 1.3 copy-done.6
  266.5 0.7 slice_reduce_fusion
  268.5 0.0 copy-done.2
  268.5 1.5 broadcast_multiply_fusion
  270.0 0.0 copy-start.5
  270.0 0.0 copy-start.7
  270.0 0.0 copy-start.9
  270.0 0.0 copy-start.10
  270.0 0.0 copy-start.12
  270.0 7.0 %multiply_subtract_fusion.1 = f32[512,1024]{1,0:T(8,128)} fusion(f32[512,1024]{1,0:T(8,128)} %param.7, bf16[1024,1024]{1,0:T(8,128)(2,1)} %broadcast_multiply_fusion, bf16[1024,1024]{1,0:T(8,128)(2,1)} %copy-done.4, f32[]{:T(128)S(6)} %div.7, bf16[1024,512]{1,0:T(8,128)(2,1)} %copy-done.11, bf16[1024,512]{1,0:T(8,128)(2,1)S(1)} %get-tuple-element.11), kind=kOutput, calls=%fused_computation.15 | convolution fusion | flops 2161115136 | bytes 10485764 | tf_op jit(solution)/shard_map/dot_general | solution.py:232
  277.0 0.0 copy-done.5
  277.0 0.0 copy-done.7
  277.0 0.0 copy-done.9
  277.0 0.0 copy-done.10
  277.0 0.0 copy-done.12
  277.1 3.8 %multiply_subtract_fusion = f32[512,1024]{1,0:T(8,128)} fusion(f32[512,1024]{1,0:T(8,128)S(1)} %copy-done.9, bf16[1024,1024]{1,0:T(8,128)(2,1)S(1)} %copy-done.10, bf16[1024,1024]{1,0:T(8,128)(2,1)S(1)} %copy-done.5, bf16[2048,512]{1,0:T(8,128)(2,1)S(1)} %copy-done.7, f32[]{:T(128)S(6)} %mul.78, f32[]{:T(128)S(6)} %div.7, ...), kind=kOutput, calls=%fused_computation.13 | convolution fusion | flops 2165309440 | bytes 12582920 | tf_op jit(solution)/shard_map/dot_general | solution.py:232
  (5 shorter events, 0.1 us)
Async XLA Ops:
  7.2 56.7 %copy-start.3 = (bf16[128,512]{1,0:T(8,128)(2,1)S(1)}, bf16[128,512]{1,0:T(8,128)(2,1)}, u32[]{:S(2)}) copy-start(bf16[128,512]{1,0:T(8,128)(2,1)} %refs_1_.1) | copy-start | bytes 393220
  7.2 56.7 %all-gather.2.cloned.1.call-start = ((), (), s32[]{:S(2)}) async-start(), calls=%async_computation | async-start | bytes 9437184 | tf_op jit(solution)/shard_map/all_gather | solution.py:243
  68.5 41.3 %copy-start.13 = (bf16[128,896]{1,0:T(8,128)(2,1)S(1)}, bf16[128,896]{1,0:T(8,128)(2,1)}, u32[]{:S(2)}) copy-start(bf16[128,896]{1,0:T(8,128)(2,1)} %param.6) | copy-start | bytes 688132
  129.6 1.6 copy-start
  170.5 1.3 copy-start.1
  178.2 16.0 %copy-start.8 = (bf16[512,1024]{1,0:T(8,128)(2,1)S(1)}, bf16[512,1024]{1,0:T(8,128)(2,1)}, u32[]{:S(2)}) copy-start(bf16[512,1024]{1,0:T(8,128)(2,1)} %convert_element_type.50) | copy-start | bytes 3145732
  194.3 24.7 %copy-start.11 = (bf16[1024,512]{1,0:T(8,128)(2,1)}, bf16[1024,512]{1,0:T(8,128)(2,1)S(1)}, u32[]{:S(2)}) copy-start(bf16[1024,512]{1,0:T(8,128)(2,1)S(1)} %neg.14) | copy-start | bytes 3145732
  219.7 48.8 %copy-start.2 = (bf16[1024,1024]{1,0:T(8,128)(2,1)S(1)}, bf16[1024,1024]{1,0:T(8,128)(2,1)}, u32[]{:S(2)}) copy-start(bf16[1024,1024]{1,0:T(8,128)(2,1)} %copy-done.1) | copy-start | bytes 6291460
  263.8 1.3 copy-start.4
  265.1 1.3 copy-start.6
  270.0 7.0 %copy-start.5 = (bf16[1024,1024]{1,0:T(8,128)(2,1)S(1)}, bf16[1024,1024]{1,0:T(8,128)(2,1)}, u32[]{:S(2)}) copy-start(bf16[1024,1024]{1,0:T(8,128)(2,1)} %copy-done.4) | copy-start | bytes 6291460
  270.0 7.0 %copy-start.7 = (bf16[2048,512]{1,0:T(8,128)(2,1)S(1)}, bf16[2048,512]{1,0:T(8,128)(2,1)}, u32[]{:S(2)}) copy-start(bf16[2048,512]{1,0:T(8,128)(2,1)} %copy-done.6) | copy-start | bytes 6291460
  270.0 7.0 %copy-start.9 = (f32[512,1024]{1,0:T(8,128)S(1)}, f32[512,1024]{1,0:T(8,128)}, u32[]{:S(2)}) copy-start(f32[512,1024]{1,0:T(8,128)} %param.7) | copy-start | bytes 6291460
  270.0 7.0 %copy-start.10 = (bf16[1024,1024]{1,0:T(8,128)(2,1)S(1)}, bf16[1024,1024]{1,0:T(8,128)(2,1)}, u32[]{:S(2)}) copy-start(bf16[1024,1024]{1,0:T(8,128)(2,1)} %broadcast_multiply_fusion) | copy-start | bytes 6291460
  270.0 7.0 %copy-start.12 = (bf16[1024,512]{1,0:T(8,128)(2,1)S(1)}, bf16[1024,512]{1,0:T(8,128)(2,1)}, u32[]{:S(2)}) copy-start(bf16[1024,512]{1,0:T(8,128)(2,1)} %copy-done.11) | copy-start | bytes 3145732
Sparse Core Ops, SparseCore 0:
  10.3 53.5 all-gather.1

commit v4 on v3

--- a/solution.py
+++ b/solution.py
@@ -222,6 +222,147 @@
     )(*arrays)
 
 
+def mix_kernel(x, out, first, held, second, piece, send, recv, dp_send, dp_recv, local_sem):
+    dp, mp = lax.axis_index("dp"), lax.axis_index("mp")
+    at = (mp // SIDE, mp % SIDE)
+    rows, half = x.shape[0], x.shape[1] // 2
+    big, small = rows // 4, rows // 16
+    few = small // N_DP
+    wide = out.shape[1] // 2
+
+    def peer(axis, k):
+        j = (at[axis] + k) % SIDE
+        return j, (dp, j * SIDE + at[1] if axis == 0 else at[0] * SIDE + j)
+
+    barrier = pltpu.get_barrier_semaphore()
+    for axis in (0, 1):
+        for k in range(1, SIDE):
+            pl.semaphore_signal(barrier, inc=1, device_id=peer(axis, k)[1], device_id_type=MESH)
+    for k in range(1, N_DP):
+        pl.semaphore_signal(barrier, inc=1, device_id=((dp + k) % N_DP, mp), device_id_type=MESH)
+    pl.semaphore_wait(barrier, 2 * (SIDE - 1) + N_DP - 1)
+
+    started = []
+
+    def send_to(src, dst, sems, index, device):
+        copy = pltpu.make_async_remote_copy(
+            src_ref=src,
+            dst_ref=dst,
+            send_sem=sems[0].at[index],
+            recv_sem=sems[1].at[index],
+            device_id=device,
+            device_id_type=MESH,
+        )
+        copy.start()
+        started.append(copy)
+        return copy
+
+    over_mp, over_dp = (send, recv), (dp_send, dp_recv)
+    order = (2, 1, 3)
+    axes = ((1, 0), (0, 1))
+    flight = {}
+
+    def index(stage, h, k):
+        return (stage * 2 + h) * 3 + k - 1
+
+    for h in range(2):
+        p, q = axes[h]
+        copies = []
+        for k in order:
+            j, device = peer(p, k)
+            src = x.at[pl.ds(pl.multiple_of(j * big, big), big), pl.ds(h * half, half)]
+            copies.append(send_to(src, first.at[h, k - 1], over_mp, index(0, h, k), device))
+        flight[0, h] = copies
+    for h in range(2):
+        p, q = axes[h]
+        for copy in flight[0, h]:
+            copy.wait_recv()
+        total = x[pl.ds(pl.multiple_of(at[p] * big, big), big), pl.ds(h * half, half)].astype(
+            jnp.float32
+        )
+        for k in range(3):
+            total += first[h, k].astype(jnp.float32)
+        held[h] = total.astype(jnp.bfloat16)
+        copies = []
+        for k in order:
+            j, device = peer(q, k)
+            src = held.at[h, pl.ds(pl.multiple_of(j * small, small), small), :]
+            copies.append(send_to(src, second.at[h, k - 1], over_mp, index(1, h, k), device))
+        flight[1, h] = copies
+    for h in range(2):
+        p, q = axes[h]
+        for copy in flight[1, h]:
+            copy.wait_recv()
+        total = held[h, pl.ds(pl.multiple_of(at[q] * small, small), small), :].astype(jnp.float32)
+        for k in range(3):
+            total += second[h, k].astype(jnp.float32)
+        piece[h] = total.astype(jnp.bfloat16)
+        tokens = pl.ds(pl.multiple_of((at[p] * SIDE + at[q]) * few, few), few)
+        landing = out.at[tokens, pl.ds(pl.multiple_of(h * wide + dp * half, half), half)]
+        own = pltpu.make_async_copy(
+            piece.at[h, pl.ds(pl.multiple_of(dp * few, few), few), :], landing, local_sem.at[h]
+        )
+        own.start()
+        copies = []
+        for k in (4, 3, 5, 2, 6, 1, 7):
+            to = (dp + k) % N_DP
+            src = piece.at[h, pl.ds(pl.multiple_of(to * few, few), few), :]
+            copies.append(send_to(src, landing, over_dp, h * 7 + k - 1, (to, mp)))
+        flight[2, h] = (own, copies)
+    for h in range(2):
+        p, q = axes[h]
+        own, copies = flight[2, h]
+        own.wait()
+        for copy in copies:
+            copy.wait_recv()
+        tokens = pl.ds(pl.multiple_of((at[p] * SIDE + at[q]) * few, few), few)
+        block = out.at[tokens, pl.ds(h * wide, wide)]
+        flight[3, h] = [
+            send_to(block, block, over_mp, index(2, h, k), peer(q, k)[1]) for k in order
+        ]
+    for h in range(2):
+        p, q = axes[h]
+        for copy in flight[3, h]:
+            copy.wait_recv()
+        tokens = pl.ds(pl.multiple_of(at[p] * SIDE * few, SIDE * few), SIDE * few)
+        block = out.at[tokens, pl.ds(h * wide, wide)]
+        flight[4, h] = [
+            send_to(block, block, over_mp, index(3, h, k), peer(p, k)[1]) for k in order
+        ]
+    for h in range(2):
+        for copy in flight[4, h]:
+            copy.wait_recv()
+    for copy in started:
+        copy.wait_send()
+
+
+def mix(x):
+    rows, columns = x.shape
+    dma = pltpu.SemaphoreType.DMA
+    half = columns // 2
+    return pl.pallas_call(
+        mix_kernel,
+        out_shape=jax.ShapeDtypeStruct((rows // N_DP, columns * N_DP), jnp.bfloat16),
+        in_specs=[pl.BlockSpec(memory_space=pltpu.VMEM)],
+        out_specs=pl.BlockSpec(memory_space=pltpu.VMEM),
+        scratch_shapes=[
+            pltpu.VMEM((2, 3, rows // 4, half), jnp.bfloat16),
+            pltpu.VMEM((2, rows // 4, half), jnp.bfloat16),
+            pltpu.VMEM((2, 3, rows // 16, half), jnp.bfloat16),
+            pltpu.VMEM((2, rows // 16, half), jnp.bfloat16),
+            dma((24,)),
+            dma((24,)),
+            dma((14,)),
+            dma((14,)),
+            dma((2,)),
+        ],
+        compiler_params=pltpu.CompilerParams(
+            collective_id=0, has_side_effects=True, vmem_limit_bytes=32 * 1024 * 1024
+        ),
+        name="sum_mixed",
+    )(x)
+
+
 def contract_cols(left, right):
     return lax.dot_general(
         left, right, (((1,), (1,)), ((), ())), preferred_element_type=jnp.float32
@@ -241,10 +382,17 @@
     tokens = rows * lax.axis_size("dp")
     rot_half = rotation.astype(jnp.bfloat16)
     rot_rows = lax.all_gather(rot_half, "dp", axis=1, tiled=True)
-    mixed_part = (jnp.dot(acts, rot_rows, preferred_element_type=jnp.float32) * inv_root).astype(
-        jnp.bfloat16
-    )
-    mixed, acts_all = communicate(0, "sum_mixed", [(mixed_part, 1)], [(acts, 1)])
+    (acts_all,) = communicate(5, "gather_acts", [], [(acts, 1)])
+    blocks = SIDE * SIDE
+    by_block = acts_all.reshape(-1, blocks, rows // blocks, acts.shape[1])
+    by_block = by_block.transpose(1, 0, 2, 3).reshape(acts_all.shape)
+    mixed_part = (
+        jnp.dot(by_block, rot_half, preferred_element_type=jnp.float32) * inv_root
+    ).astype(jnp.bfloat16)
+    mixed = mix(mixed_part)
+    run = mixed.shape[1] // (2 * N_DP)
+    starts = [(h * N_DP + d) * run for d in range(N_DP) for h in range(2)]
+    mixed = jnp.concatenate([mixed[:, start : start + run] for start in starts], axis=1)
     hidden = jnp.dot(mixed, w_up, preferred_element_type=jnp.float32)
     sigmoid_hidden = jax.nn.sigmoid(hidden)
     grad_hidden = (

time: 288 us -> 260 us (0.903)
  waiting for transfers between devices: 53.9 us -> 0.02 us
  Pallas kernels: 163 us -> 190 us
  matrix products: 44.3 us -> 40.3 us
    all_gather x1, waiting for transfers between devices: 53.8 us -> 0.01 us  [local(): rot_rows = lax.all_gather(rot_half, 'dp', axis=1, tiled=True)]
    pallas_call x0 -> x1, Pallas kernels: none -> 47.7 us  [mix(): pl.pallas_call(mix_kernel, out_shape=jax.ShapeDtypeStruct((rows // N_DP,...]
    pallas_call x5, Pallas kernels: 163 us -> 142 us  [communicate(): pl.pallas_call(functools.partial(kernel, dims, len(moves), modes), out_sh...]
    dot_general x1, matrix products: 4.69 us -> 1.27 us  [local(): jnp.dot(by_block, rot_half, preferred_element_type=jnp.float32) * inv_root]
    unnamed x28 -> x43, local copies, waits for them, and re-layouts: 5.6 us -> 6.39 us
  transfers between devices with their start and end apart: 1 -> 1, of which waited for: 1 -> 0; matrix products, arithmetic and copies ran while one was open for 0% -> 9% of each run, Pallas kernels for 0% -> 42%
where the time goes in v4:
time: 260 us
  Pallas kernels  190 us (73%)
  matrix products  40.3 us (15%)
  between operations  15.7 us (6%)
  other arithmetic  6.9 us (3%)
  local copies, waits for them, and re-layouts  6.52 us (3%)
    pallas_call x5, Pallas kernels, communicate(): pl.pallas_call(functools.partial(kernel, dims, len(moves), modes), out_sh...  142 us
    pallas_call x1, Pallas kernels, mix(): pl.pallas_call(mix_kernel, out_shape=jax.ShapeDtypeStruct((rows // N_DP,...  47.7 us
    dot_general x3, matrix products, contract_cols(): lax.dot_general(left, right, (((1,), (1,)), ((), ())), preferred_element_...  26.9 us
    dot_general x3, matrix products, contract_rows(): lax.dot_general(left, right, (((0,), (0,)), ((), ())), preferred_element_...  10.8 us
    unnamed x43, local copies, waits for them, and re-layouts  6.39 us
  transfers between devices with their start and end apart: 1, of which 0 were waited for; matrix products, arithmetic and copies ran while one was open for 9% of the time, Pallas kernels for 42%

profile of v4, /device:TPU:1, one launch (start us, length us, event | category | flops | bytes accessed | tf_op | source)
XLA Modules:
  0.0 259.6 jit_solution(17567498706504508181)
XLA Ops:
  7.2 0.0 copy-start.4
  7.2 0.0 all-gather.2.cloned.1.call-start
  7.2 2.9 %convert_element_type.50 = bf16[512,1024]{1,0:T(8,128)(2,1)} convert(f32[512,1024]{1,0:T(8,128)} %param.7) | non-fusion elementwise | flops 524288 | bytes 3145728 | tf_op jit(solution)/shard_map/convert_element_type | solution.py:383
  10.1 0.0 copy-start.7
  10.1 0.0 all-gather.2.cloned.1.call-update
  10.1 0.0 copy-done.4
  10.1 20.4 %gather_acts.1 = bf16[1024,512]{1,0:T(8,128)(2,1)S(1)} custom-call(bf16[128,512]{1,0:T(8,128)(2,1)S(1)} %copy-done.4), custom_call_target="tpu_custom_call" | custom-call | tf_op jit(solution)/shard_map/gather_acts/pallas_call | solution.py:203
  30.5 0.1 copy.6
  30.6 0.0 copy-done.7
  30.7 1.3 multiply_convert_fusion.1.x
  31.9 47.7 %sum_mixed.1 = bf16[128,8192]{1,0:T(8,128)(2,1)S(1)} custom-call(bf16[1024,1024]{1,0:T(8,128)(2,1)S(1)} %multiply_convert_fusion.1.x), custom_call_target="tpu_custom_call" | custom-call | tf_op jit(solution)/shard_map/sum_mixed/pallas_call | solution.py:343
  79.7 0.0 copy-start.13
  80.0 0.6 copy-done.13
  80.6 19.8 %convolution_convert_fusion.refs_0_ = bf16[128,8192]{1,0:T(8,128)(2,1)} fusion(bf16[8192,896]{1,0:T(8,128)(2,1)} %param.5, bf16[128,896]{1,0:T(8,128)(2,1)S(1)} %copy-done.13, bf16[128,8192]{1,0:T(8,128)(2,1)S(1)} %slice_dynamic-update-slice_fusion.refs_1_), kind=kOutput, calls=%fused_computation | convolution fusion | flops 3760291840 | bytes 19103744 | tf_op jit(solution)/shard_map/dot_general | solution.py:367
  100.4 0.0 copy-start
  100.4 1.6 copy-done
  102.0 41.1 %sum_grad.1 = (bf16[128,8192]{1,0:T(8,128)(2,1)S(1)}, bf16[1024,1024]{1,0:T(8,128)(2,1)S(1)}) custom-call(bf16[128,8192]{1,0:T(8,128)(2,1)S(1)} %copy-done, bf16[128,8192]{1,0:T(8,128)(2,1)S(1)} %slice_dynamic-update-slice_fusion.refs_1_), custom_call_target="tpu_custom_call" | custom-call | tf_op jit(solution)/shard_map/sum_grad/pallas_call | solution.py:203
  143.1 0.0 copy-start.1
  143.1 1.3 copy-done.1
  144.4 0.0 copy-start.2
  144.4 1.3 copy-done.2
  145.7 0.0 copy-start.3
  145.7 3.2 %broadcast_multiply_fusion = bf16[1024,1024]{1,0:T(8,128)(2,1)} fusion(bf16[1024,1024]{1,0:T(8,128)(2,1)} %copy-done.1), kind=kLoop, calls=%fused_computation.17 | loop fusion | flops 1048576 | bytes 4194304 | tf_op jit(solution)/shard_map/mul | solution.py:403
  148.9 0.0 copy-done.3
  148.9 6.4 %fusion.15 = (bf16[128,512]{1,0:T(8,128)(2,1)S(1)}, bf16[128,512]{1,0:T(8,128)(2,1)S(1)}) fusion(bf16[128,8192]{1,0:T(8,128)(2,1)S(1)} %copy-done.3, bf16[512,8192]{1,0:T(8,128)(2,1)} %all-gather.2.cloned.1.call-done), kind=kOutput, calls=%fused_computation.50 | convolution fusion | flops 1073872896 | bytes 10747904 | tf_op jit(solution)/shard_map/dot_general | solution.py:367
  155.3 15.5 %gather_factor.1 = bf16[1024,512]{1,0:T(8,128)(2,1)S(1)} custom-call(bf16[128,512]{1,0:T(8,128)(2,1)S(1)} %get-tuple-element.17.refs_0_), custom_call_target="tpu_custom_call" | custom-call | tf_op jit(solution)/shard_map/gather_factor/pallas_call | solution.py:203
  170.8 0.0 copy-done.8
  170.8 1.3 multiply_convert_fusion.refs_0_
  172.1 0.2 neg.14
  172.3 0.0 copy-start.11
  172.3 0.7 convolution_convert_fusion.1.refs_0_
  173.1 20.8 %sum_gram.1 = bf16[2048,256]{1,0:T(8,128)(2,1)S(1)} custom-call(bf16[2048,256]{1,0:T(8,128)(2,1)S(1)} %convolution_convert_fusion.1.refs_0_), custom_call_target="tpu_custom_call" | custom-call | tf_op jit(solution)/shard_map/sum_gram/pallas_call | solution.py:203
  193.9 0.0 copy-done.11
  193.9 0.7 convolution_convert_fusion.2.refs_1_
  194.7 44.5 %sum_left.1 = (bf16[1024,1024]{1,0:T(8,128)(2,1)S(1)}, bf16[2048,512]{1,0:T(8,128)(2,1)S(1)}, bf16[128,256]{1,0:T(8,128)(2,1)S(1)}) custom-call(bf16[1024,1024]{1,0:T(8,128)(2,1)S(1)} %multiply_convert_fusion.refs_0_, bf16[256,512]{1,0:T(8,128)(2,1)S(1)} %convolution_convert_fusion.2.refs_1_, bf16[16,256]{1,0:T(8,128)(2,1)S(1)} %broadcast_in_dim.3.refs_2_), custom_call_target="tpu_custom_call" | custom-call | tf_op jit(solution)/shard_map/sum_left/pallas_call | solution.py:203
  239.3 0.0 copy-start.5
  239.3 1.3 copy-done.5
  240.7 0.6 slice_reduce_fusion
  242.6 0.0 copy-start.6
  242.6 0.0 copy-start.9
  242.6 0.0 copy-start.10
  242.6 0.0 copy-start.12
  242.6 6.4 %multiply_subtract_fusion.1 = f32[512,1024]{1,0:T(8,128)} fusion(f32[512,1024]{1,0:T(8,128)} %param.7, bf16[1024,1024]{1,0:T(8,128)(2,1)} %broadcast_multiply_fusion, bf16[1024,1024]{1,0:T(8,128)(2,1)S(1)} %get-tuple-element.9, f32[]{:T(128)S(6)} %div.7, bf16[1024,512]{1,0:T(8,128)(2,1)} %copy-done.11, bf16[1024,512]{1,0:T(8,128)(2,1)S(1)} %gather_acts.1), kind=kOutput, calls=%fused_computation.14 | convolution fusion | flops 2161115136 | bytes 10485764 | tf_op jit(solution)/shard_map/dot_general | solution.py:373
  249.0 0.0 copy-done.6
  249.0 0.0 copy-done.9
  249.0 0.0 copy-done.10
  249.0 0.0 copy-done.12
  249.0 3.8 %multiply_subtract_fusion = f32[512,1024]{1,0:T(8,128)} fusion(f32[512,1024]{1,0:T(8,128)S(1)} %copy-done.9, bf16[1024,1024]{1,0:T(8,128)(2,1)S(1)} %copy-done.10, bf16[1024,1024]{1,0:T(8,128)(2,1)S(1)} %get-tuple-element.9, bf16[2048,512]{1,0:T(8,128)(2,1)S(1)} %copy-done.6, f32[]{:T(128)S(6)} %mul.78, f32[]{:T(128)S(6)} %div.7, ...), kind=kOutput, calls=%fused_computation.12 | convolution fusion | flops 2165309440 | bytes 12582920 | tf_op jit(solution)/shard_map/dot_general | solution.py:373
  (23 shorter events, 0.3 us)
Async XLA Ops:
  7.2 2.9 %copy-start.4 = (bf16[128,512]{1,0:T(8,128)(2,1)S(1)}, bf16[128,512]{1,0:T(8,128)(2,1)}, u32[]{:S(2)}) copy-start(bf16[128,512]{1,0:T(8,128)(2,1)} %refs_0_.1) | copy-start | bytes 393220
  7.2 141.7 %all-gather.2.cloned.1.call-start = ((), (), s32[]{:S(2)}) async-start(), calls=%async_computation | async-start | bytes 9437184 | tf_op jit(solution)/shard_map/all_gather | solution.py:384
  10.1 20.6 %copy-start.7 = (bf16[512,1024]{1,0:T(8,128)(2,1)S(1)}, bf16[512,1024]{1,0:T(8,128)(2,1)}, u32[]{:S(2)}) copy-start(bf16[512,1024]{1,0:T(8,128)(2,1)} %convert_element_type.50) | copy-start | bytes 3145732
  79.7 0.9 copy-start.13
  100.4 1.6 copy-start
  143.1 1.3 copy-start.1
  144.4 1.3 copy-start.2
  145.7 3.2 %copy-start.3 = (bf16[128,8192]{1,0:T(8,128)(2,1)S(1)}, bf16[128,8192]{1,0:T(8,128)(2,1)}, u32[]{:S(2)}) copy-start(bf16[128,8192]{1,0:T(8,128)(2,1)} %copy-done.2) | copy-start | bytes 6291460
  148.9 21.9 %copy-start.8 = (bf16[512,1024]{1,0:T(8,128)(2,1)S(1)}, bf16[512,1024]{1,0:T(8,128)(2,1)}, u32[]{:S(2)}) copy-start(bf16[512,1024]{1,0:T(8,128)(2,1)} %convert_element_type.50) | copy-start | bytes 3145732
  172.3 21.6 %copy-start.11 = (bf16[1024,512]{1,0:T(8,128)(2,1)}, bf16[1024,512]{1,0:T(8,128)(2,1)S(1)}, u32[]{:S(2)}) copy-start(bf16[1024,512]{1,0:T(8,128)(2,1)S(1)} %neg.14) | copy-start | bytes 3145732
  239.3 1.3 copy-start.5
  242.6 6.4 %copy-start.6 = (bf16[2048,512]{1,0:T(8,128)(2,1)S(1)}, bf16[2048,512]{1,0:T(8,128)(2,1)}, u32[]{:S(2)}) copy-start(bf16[2048,512]{1,0:T(8,128)(2,1)} %copy-done.5) | copy-start | bytes 6291460
  242.6 6.4 %copy-start.9 = (f32[512,1024]{1,0:T(8,128)S(1)}, f32[512,1024]{1,0:T(8,128)}, u32[]{:S(2)}) copy-start(f32[512,1024]{1,0:T(8,128)} %param.7) | copy-start | bytes 6291460
  242.6 6.4 %copy-start.10 = (bf16[1024,1024]{1,0:T(8,128)(2,1)S(1)}, bf16[1024,1024]{1,0:T(8,128)(2,1)}, u32[]{:S(2)}) copy-start(bf16[1024,1024]{1,0:T(8,128)(2,1)} %broadcast_multiply_fusion) | copy-start | bytes 6291460
  242.6 6.4 %copy-start.12 = (bf16[1024,512]{1,0:T(8,128)(2,1)S(1)}, bf16[1024,512]{1,0:T(8,128)(2,1)}, u32[]{:S(2)}) copy-start(bf16[1024,512]{1,0:T(8,128)(2,1)} %copy-done.11) | copy-start | bytes 3145732
Sparse Core Ops, SparseCore 0:
  10.2 55.2 all-gather.1

commit v5 on v4

--- a/solution.py
+++ b/solution.py
@@ -398,16 +398,16 @@
     grad_hidden = (
         out_grad.astype(jnp.float32) * sigmoid_hidden * (1.0 + hidden * (1.0 - sigmoid_hidden))
     ).astype(jnp.bfloat16)
+    grad_hidden = lax.optimization_barrier(grad_hidden)
     grad_part = contract_cols(grad_hidden, w_up).astype(jnp.bfloat16)
     grad_mixed, right = communicate(1, "sum_grad", [(grad_part, 1)], [(mixed, "transpose")])
-    right = 2 * right
     factor = contract_cols(grad_mixed, rot_rows).astype(jnp.bfloat16)
     (factor_all,) = communicate(2, "gather_factor", [], [(factor, 1)])
     spread_rows = jnp.concatenate((factor_all, acts_all), axis=0)
     skew_rows = jnp.concatenate((acts_all, -factor_all), axis=0)
     own = jnp.concatenate((acts, -factor), axis=0)
     left_part = (
-        jnp.dot(factor_all, rot_half, preferred_element_type=jnp.float32) * (2 * inv_root)
+        jnp.dot(factor_all, rot_half, preferred_element_type=jnp.float32) * inv_root
     ).astype(jnp.bfloat16)
     gram_part = contract_cols(spread_rows, own).astype(jnp.bfloat16)
     (gram,) = communicate(3, "sum_gram", [(gram_part, 0)], [])
@@ -435,8 +435,8 @@
         skew_rows.astype(jnp.float32) - (step_size * inv_root) * second_all.astype(jnp.float32)
     ).astype(jnp.bfloat16)
     sides = jnp.concatenate((left, right), axis=0)
-    half = rotation - step_size * contract_rows(skew_rows, sides)
-    full = rotation - step_size * contract_rows(second_map, sides)
+    half = rotation - (2 * step_size) * contract_rows(skew_rows, sides)
+    full = rotation - (2 * step_size) * contract_rows(second_map, sides)
     return half, full
 
 

time: 260 us -> 249 us (0.958)
  matrix products: 40.3 us -> 30.6 us
  other arithmetic: 6.9 us -> 3.73 us
    dot_general x3, matrix products: 26.9 us -> 17.6 us  [contract_cols(): lax.dot_general(left, right, (((1,), (1,)), ((), ())), preferred_element_...]
    mul x1 -> x0, other arithmetic: 3.19 us -> none  [local(): right = 2 * right]
    dot_general x3, matrix products: 10.8 us -> 8.09 us  [contract_rows(): lax.dot_general(left, right, (((0,), (0,)), ((), ())), preferred_element_...]
    unnamed x43 -> x40, local copies, waits for them, and re-layouts: 6.39 us -> 8.01 us
  transfers between devices with their start and end apart: 1 -> 1, of which waited for: 0 -> 0; matrix products, arithmetic and copies ran while one was open for 9% -> 6% of each run, Pallas kernels for 42% -> 44%
where the time goes in v5:
time: 249 us
  Pallas kernels  190 us (76%)
  matrix products  30.6 us (12%)
  between operations  15.7 us (6%)
  local copies, waits for them, and re-layouts  8.33 us (3%)
  other arithmetic  3.73 us (1%)
    pallas_call x5, Pallas kernels, communicate(): pl.pallas_call(functools.partial(kernel, dims, len(moves), modes), out_sh...  142 us
    pallas_call x1, Pallas kernels, mix(): pl.pallas_call(mix_kernel, out_shape=jax.ShapeDtypeStruct((rows // N_DP,...  47.7 us
    dot_general x3, matrix products, contract_cols(): lax.dot_general(left, right, (((1,), (1,)), ((), ())), preferred_element_...  17.6 us
    dot_general x3, matrix products, contract_rows(): lax.dot_general(left, right, (((0,), (0,)), ((), ())), preferred_element_...  8.09 us
    unnamed x40, local copies, waits for them, and re-layouts  8.01 us
  transfers between devices with their start and end apart: 1, of which 0 were waited for; matrix products, arithmetic and copies ran while one was open for 6% of the time, Pallas kernels for 44%

profile of v5, /device:TPU:1, one launch (start us, length us, event | category | flops | bytes accessed | tf_op | source)
XLA Modules:
  0.0 248.6 jit_solution(8483641339914679426)
XLA Ops:
  7.2 0.0 copy-start.3
  7.2 0.0 all-gather.2.cloned.1.call-start
  7.2 2.8 %convert_element_type.50 = bf16[512,1024]{1,0:T(8,128)(2,1)} convert(f32[512,1024]{1,0:T(8,128)} %param.7) | non-fusion elementwise | flops 524288 | bytes 3145728 | tf_op jit(solution)/shard_map/convert_element_type | solution.py:383
  10.1 0.0 copy-start.7
  10.1 0.0 all-gather.2.cloned.1.call-update
  10.1 0.0 copy-done.3
  10.1 20.4 %gather_acts.1 = bf16[1024,512]{1,0:T(8,128)(2,1)S(1)} custom-call(bf16[128,512]{1,0:T(8,128)(2,1)S(1)} %copy-done.3), custom_call_target="tpu_custom_call" | custom-call | tf_op jit(solution)/shard_map/gather_acts/pallas_call | solution.py:203
  30.5 0.1 copy.6
  30.6 0.0 copy-done.7
  30.7 0.0 copy-start.6
  30.7 1.3 multiply_convert_fusion.1.x
  31.9 47.7 %sum_mixed.1 = bf16[128,8192]{1,0:T(8,128)(2,1)S(1)} custom-call(bf16[1024,1024]{1,0:T(8,128)(2,1)S(1)} %multiply_convert_fusion.1.x), custom_call_target="tpu_custom_call" | custom-call | tf_op jit(solution)/shard_map/sum_mixed/pallas_call | solution.py:343
  79.6 0.0 copy-start.11
  80.0 0.0 copy-done.6
  80.0 0.6 copy-done.11
  80.6 2.5 multiply_convert_fusion.2
  83.1 9.9 %convolution_convert_fusion.refs_0_ = bf16[128,8192]{1,0:T(8,128)(2,1)S(1)} fusion(bf16[128,896]{1,0:T(8,128)(2,1)S(1)} %multiply_convert_fusion.2, bf16[8192,896]{1,0:T(8,128)(2,1)} %param.5), kind=kOutput, calls=%fused_computation | convolution fusion | flops 1880096768 | bytes 17006592 | tf_op jit(solution)/shard_map/dot_general | solution.py:367
  93.0 41.4 %sum_grad.1 = (bf16[128,8192]{1,0:T(8,128)(2,1)S(1)}, bf16[1024,1024]{1,0:T(8,128)(2,1)S(1)}) custom-call(bf16[128,8192]{1,0:T(8,128)(2,1)S(1)} %convolution_convert_fusion.refs_0_, bf16[128,8192]{1,0:T(8,128)(2,1)S(1)} %slice_dynamic-update-slice_fusion.refs_1_), custom_call_target="tpu_custom_call" | custom-call | tf_op jit(solution)/shard_map/sum_grad/pallas_call | solution.py:203
  134.3 0.0 copy-start
  134.4 1.3 copy-done
  135.7 0.0 copy-start.2
  135.7 1.3 copy-done.2
  137.0 0.0 all-gather.2.cloned.1.call-done
  137.0 6.9 %fusion.12 = (bf16[128,512]{1,0:T(8,128)(2,1)S(1)}, bf16[128,512]{1,0:T(8,128)(2,1)S(1)}) fusion(bf16[128,8192]{1,0:T(8,128)(2,1)} %copy-done.2, bf16[512,8192]{1,0:T(8,128)(2,1)} %all-gather.2.cloned.1.call-done), kind=kOutput, calls=%fused_computation.47 | convolution fusion | flops 1073872896 | bytes 10747904 | tf_op jit(solution)/shard_map/dot_general | solution.py:367
  143.9 15.4 %gather_factor.1 = bf16[1024,512]{1,0:T(8,128)(2,1)S(1)} custom-call(bf16[128,512]{1,0:T(8,128)(2,1)S(1)} %get-tuple-element.17.refs_0_), custom_call_target="tpu_custom_call" | custom-call | tf_op jit(solution)/shard_map/gather_factor/pallas_call | solution.py:203
  159.4 0.2 neg.14
  159.6 0.0 copy-start.9
  159.6 1.3 multiply_convert_fusion.refs_0_
  160.8 0.7 convolution_convert_fusion.1.refs_0_
  161.6 21.5 %sum_gram.1 = bf16[2048,256]{1,0:T(8,128)(2,1)S(1)} custom-call(bf16[2048,256]{1,0:T(8,128)(2,1)S(1)} %convolution_convert_fusion.1.refs_0_), custom_call_target="tpu_custom_call" | custom-call | tf_op jit(solution)/shard_map/sum_gram/pallas_call | solution.py:203
  183.1 0.0 copy-done.9
  183.1 0.7 convolution_convert_fusion.2.refs_1_
  183.9 43.8 %sum_left.1 = (bf16[1024,1024]{1,0:T(8,128)(2,1)S(1)}, bf16[2048,512]{1,0:T(8,128)(2,1)S(1)}, bf16[128,256]{1,0:T(8,128)(2,1)S(1)}) custom-call(bf16[1024,1024]{1,0:T(8,128)(2,1)S(1)} %multiply_convert_fusion.refs_0_, bf16[256,512]{1,0:T(8,128)(2,1)S(1)} %convolution_convert_fusion.2.refs_1_, bf16[16,256]{1,0:T(8,128)(2,1)S(1)} %broadcast_in_dim.3.refs_2_), custom_call_target="tpu_custom_call" | custom-call | tf_op jit(solution)/shard_map/sum_left/pallas_call | solution.py:203
  227.7 0.0 copy-start.4
  227.7 1.3 copy-done.4
  229.0 0.6 slice_reduce_fusion
  231.0 0.0 copy-start.1
  231.0 0.2 constant_dynamic-update-slice_fusion.1
  231.2 1.4 copy-done.1
  232.6 0.0 copy-start.8
  232.6 0.0 copy-start.10
  232.6 0.2 constant_dynamic-update-slice_fusion
  232.7 1.4 copy-done.8
  234.1 0.3 copy-done.10
  234.4 0.0 copy-start.5
  234.4 3.7 %multiply_subtract_fusion.1 = f32[512,1024]{1,0:T(8,128)} fusion(f32[512,1024]{1,0:T(8,128)S(1)} %copy-done.8, bf16[2048,1024]{1,0:T(8,128)(2,1)S(1)} %constant_dynamic-update-slice_fusion, f32[]{:T(128)S(6)} %mul.64, bf16[1024,512]{1,0:T(8,128)(2,1)S(1)} %copy-done.10, bf16[1024,512]{1,0:T(8,128)(2,1)S(1)} %gather_acts.1), kind=kOutput, calls=%fused_computation.12 | convolution fusion | flops 2152726528 | bytes 10485764 | tf_op jit(solution)/shard_map/dot_general | solution.py:373
  238.1 0.0 copy-done.5
  238.1 3.7 %multiply_subtract_fusion = f32[512,1024]{1,0:T(8,128)} fusion(f32[512,1024]{1,0:T(8,128)S(1)} %copy-done.8, bf16[2048,1024]{1,0:T(8,128)(2,1)S(1)} %constant_dynamic-update-slice_fusion, bf16[2048,512]{1,0:T(8,128)(2,1)S(1)} %copy-done.5, f32[]{:T(128)S(6)} %mul.67, f32[]{:T(128)S(6)} %mul.64, bf16[1024,512]{1,0:T(8,128)(2,1)S(1)} %copy-done.10, ...), kind=kOutput, calls=%fused_computation.10 | convolution fusion | flops 2156920832 | bytes 12582920 | tf_op jit(solution)/shard_map/dot_general | solution.py:373
  (21 shorter events, 0.3 us)
Async XLA Ops:
  7.2 2.9 %copy-start.3 = (bf16[128,512]{1,0:T(8,128)(2,1)S(1)}, bf16[128,512]{1,0:T(8,128)(2,1)}, u32[]{:S(2)}) copy-start(bf16[128,512]{1,0:T(8,128)(2,1)} %refs_0_.1) | copy-start | bytes 393220
  7.2 129.8 %all-gather.2.cloned.1.call-start = ((), (), s32[]{:S(2)}) async-start(), calls=%async_computation | async-start | bytes 9437184 | tf_op jit(solution)/shard_map/all_gather | solution.py:384
  10.1 20.6 %copy-start.7 = (bf16[512,1024]{1,0:T(8,128)(2,1)S(1)}, bf16[512,1024]{1,0:T(8,128)(2,1)}, u32[]{:S(2)}) copy-start(bf16[512,1024]{1,0:T(8,128)(2,1)} %convert_element_type.50) | copy-start | bytes 3145732
  30.7 49.3 %copy-start.6 = (bf16[8192,896]{1,0:T(8,128)(2,1)S(1)}, bf16[8192,896]{1,0:T(8,128)(2,1)}, u32[]{:S(2)}) copy-start(bf16[8192,896]{1,0:T(8,128)(2,1)} %param.5) | copy-start | bytes 44040196
  79.6 0.9 copy-start.11
  134.3 1.3 copy-start
  135.7 1.3 copy-start.2
  159.6 23.5 %copy-start.9 = (bf16[1024,512]{1,0:T(8,128)(2,1)}, bf16[1024,512]{1,0:T(8,128)(2,1)S(1)}, u32[]{:S(2)}) copy-start(bf16[1024,512]{1,0:T(8,128)(2,1)S(1)} %neg.14) | copy-start | bytes 3145732
  227.7 1.3 copy-start.4
  231.0 1.6 copy-start.1
  232.6 1.6 copy-start.8
  232.6 1.9 copy-start.10
  234.4 3.7 %copy-start.5 = (bf16[2048,512]{1,0:T(8,128)(2,1)S(1)}, bf16[2048,512]{1,0:T(8,128)(2,1)}, u32[]{:S(2)}) copy-start(bf16[2048,512]{1,0:T(8,128)(2,1)} %copy-done.4) | copy-start | bytes 6291460
Sparse Core Ops, SparseCore 0:
  10.2 55.2 all-gather.1

commit v6 on v5

--- a/solution.py
+++ b/solution.py
@@ -95,7 +95,8 @@
                 )
             )
         flight[0, h, a] = copies
-    exchanges = []
+    exchanges, relays = [], []
+    partner = dp + 1 - 2 * (dp % 2)
     for i, mode in enumerate(modes):
         which, block, blocks, split = mode
         rows = ys[which].shape[0] // blocks
@@ -111,8 +112,8 @@
         own = pltpu.make_async_copy(part(dp), landing, local_sem.at[i])
         own.start()
         exchanges.append(own)
-        for k in (4, 3, 5, 2, 6, 1, 7):
-            to = (dp + k) % N_DP
+        for k in (4, 3, 5, 2, 6, 1, 7) if split else (4, 2, 6, 1):
+            to = (dp + k) % N_DP if k > 1 or split else partner
             copy = pltpu.make_async_remote_copy(
                 src_ref=part(to),
                 dst_ref=landing,
@@ -122,7 +123,10 @@
                 device_id_type=MESH,
             )
             copy.start()
-            exchanges.append(copy)
+            if split or k == 1:
+                exchanges.append(copy)
+            else:
+                relays.append((i, k, copy))
     for h, a in todo:
         p, q, base, big, small = spot(a, h)
         for copy in flight[0, h, a]:
@@ -168,6 +172,22 @@
         flight[3, h, a] = [
             send_to(block, block, index(3, h, a, k), peer(p, k)[1]) for k in order
         ]
+    for i, k, copy in relays:
+        copy.wait()
+        which, block, blocks, split = modes[i]
+        rows = ys[which].shape[0] // blocks
+        origin = (dp + N_DP - k) % N_DP
+        there = outs[which].at[pl.ds(pl.multiple_of((block * N_DP + origin) * rows, rows), rows), :]
+        onward = pltpu.make_async_remote_copy(
+            src_ref=there,
+            dst_ref=there,
+            send_sem=dp_send.at[i * 7 + k],
+            recv_sem=dp_recv.at[i * 7 + k],
+            device_id=(partner, mp),
+            device_id_type=MESH,
+        )
+        onward.start()
+        exchanges.append(onward)
     for h, a in todo:
         for copy in flight[3, h, a]:
             copy.wait_recv()

time: 249 us -> 238 us (0.956)
  Pallas kernels: 190 us -> 179 us
    pallas_call x5, Pallas kernels: 142 us -> 131 us  [communicate(): pl.pallas_call(functools.partial(kernel, dims, len(moves), modes), out_sh...]
  transfers between devices with their start and end apart: 1 -> 1, of which waited for: 0 -> 0; matrix products, arithmetic and copies ran while one was open for 6% -> 6% of each run, Pallas kernels for 44% -> 43%
where the time goes in v6:
time: 238 us
  Pallas kernels  179 us (75%)
  matrix products  30.7 us (13%)
  between operations  15.7 us (7%)
  local copies, waits for them, and re-layouts  8.33 us (4%)
  other arithmetic  3.73 us (2%)
    pallas_call x5, Pallas kernels, communicate(): pl.pallas_call(functools.partial(kernel, dims, len(moves), modes), out_sh...  131 us
    pallas_call x1, Pallas kernels, mix(): pl.pallas_call(mix_kernel, out_shape=jax.ShapeDtypeStruct((rows // N_DP,...  47.6 us
    dot_general x3, matrix products, contract_cols(): lax.dot_general(left, right, (((1,), (1,)), ((), ())), preferred_element_...  17.6 us
    dot_general x3, matrix products, contract_rows(): lax.dot_general(left, right, (((0,), (0,)), ((), ())), preferred_element_...  8.09 us
    unnamed x40, local copies, waits for them, and re-layouts  8.01 us
  transfers between devices with their start and end apart: 1, of which 0 were waited for; matrix products, arithmetic and copies ran while one was open for 6% of the time, Pallas kernels for 43%

profile of v6, /device:TPU:1, one launch (start us, length us, event | category | flops | bytes accessed | tf_op | source)
XLA Modules:
  0.0 237.5 jit_solution(6177838861759608650)
XLA Ops:
  7.2 0.0 copy-start.3
  7.2 0.0 all-gather.2.cloned.1.call-start
  7.2 2.8 %convert_element_type.50 = bf16[512,1024]{1,0:T(8,128)(2,1)} convert(f32[512,1024]{1,0:T(8,128)} %param.7) | non-fusion elementwise | flops 524288 | bytes 3145728 | tf_op jit(solution)/shard_map/convert_element_type | solution.py:403
  10.1 0.0 copy-start.7
  10.1 0.0 all-gather.2.cloned.1.call-update
  10.1 0.0 copy-done.3
  10.1 14.3 %gather_acts.1 = bf16[1024,512]{1,0:T(8,128)(2,1)S(1)} custom-call(bf16[128,512]{1,0:T(8,128)(2,1)S(1)} %copy-done.3), custom_call_target="tpu_custom_call" | custom-call | tf_op jit(solution)/shard_map/gather_acts/pallas_call | solution.py:223
  24.4 0.1 copy.6
  24.5 0.0 copy-done.7
  24.5 0.0 copy-start.6
  24.6 1.3 multiply_convert_fusion.1.x
  25.8 47.6 %sum_mixed.1 = bf16[128,8192]{1,0:T(8,128)(2,1)S(1)} custom-call(bf16[1024,1024]{1,0:T(8,128)(2,1)S(1)} %multiply_convert_fusion.1.x), custom_call_target="tpu_custom_call" | custom-call | tf_op jit(solution)/shard_map/sum_mixed/pallas_call | solution.py:363
  73.4 0.0 copy-start.11
  73.7 0.0 copy-done.6
  73.8 0.6 copy-done.11
  74.4 2.5 %multiply_convert_fusion.2 = bf16[128,896]{1,0:T(8,128)(2,1)S(1)} fusion(bf16[128,896]{1,0:T(8,128)(2,1)S(1)} %copy-done.11, bf16[128,8192]{1,0:T(8,128)(2,1)S(1)} %slice_dynamic-update-slice_fusion.refs_1_, bf16[8192,896]{1,0:T(8,128)(2,1)S(1)} %copy-done.6), kind=kOutput, calls=%fused_computation.15 | convolution fusion | flops 1880195072 | bytes 17235968 | tf_op jit(solution)/shard_map/dot_general | solution.py:416
  76.8 9.9 %convolution_convert_fusion.refs_0_ = bf16[128,8192]{1,0:T(8,128)(2,1)S(1)} fusion(bf16[128,896]{1,0:T(8,128)(2,1)S(1)} %multiply_convert_fusion.2, bf16[8192,896]{1,0:T(8,128)(2,1)} %param.5), kind=kOutput, calls=%fused_computation | convolution fusion | flops 1880096768 | bytes 17006592 | tf_op jit(solution)/shard_map/dot_general | solution.py:387
  86.8 40.9 %sum_grad.1 = (bf16[128,8192]{1,0:T(8,128)(2,1)S(1)}, bf16[1024,1024]{1,0:T(8,128)(2,1)S(1)}) custom-call(bf16[128,8192]{1,0:T(8,128)(2,1)S(1)} %convolution_convert_fusion.refs_0_, bf16[128,8192]{1,0:T(8,128)(2,1)S(1)} %slice_dynamic-update-slice_fusion.refs_1_), custom_call_target="tpu_custom_call" | custom-call | tf_op jit(solution)/shard_map/sum_grad/pallas_call | solution.py:223
  127.7 0.0 copy-start
  127.7 1.3 copy-done
  129.0 0.0 copy-start.2
  129.0 1.3 copy-done.2
  130.3 0.0 all-gather.2.cloned.1.call-done
  130.3 6.9 %fusion.12 = (bf16[128,512]{1,0:T(8,128)(2,1)S(1)}, bf16[128,512]{1,0:T(8,128)(2,1)S(1)}) fusion(bf16[128,8192]{1,0:T(8,128)(2,1)} %copy-done.2, bf16[512,8192]{1,0:T(8,128)(2,1)} %all-gather.2.cloned.1.call-done), kind=kOutput, calls=%fused_computation.47 | convolution fusion | flops 1073872896 | bytes 10747904 | tf_op jit(solution)/shard_map/dot_general | solution.py:387
  137.3 12.0 %gather_factor.1 = bf16[1024,512]{1,0:T(8,128)(2,1)S(1)} custom-call(bf16[128,512]{1,0:T(8,128)(2,1)S(1)} %get-tuple-element.17.refs_0_), custom_call_target="tpu_custom_call" | custom-call | tf_op jit(solution)/shard_map/gather_factor/pallas_call | solution.py:223
  149.3 0.2 neg.14
  149.5 0.0 copy-start.9
  149.5 1.3 multiply_convert_fusion.refs_0_
  150.7 0.7 convolution_convert_fusion.1.refs_0_
  151.5 23.8 %sum_gram.1 = bf16[2048,256]{1,0:T(8,128)(2,1)S(1)} custom-call(bf16[2048,256]{1,0:T(8,128)(2,1)S(1)} %convolution_convert_fusion.1.refs_0_), custom_call_target="tpu_custom_call" | custom-call | tf_op jit(solution)/shard_map/sum_gram/pallas_call | solution.py:223
  175.2 0.0 copy-done.9
  175.3 0.7 convolution_convert_fusion.2.refs_1_
  176.1 40.5 %sum_left.1 = (bf16[1024,1024]{1,0:T(8,128)(2,1)S(1)}, bf16[2048,512]{1,0:T(8,128)(2,1)S(1)}, bf16[128,256]{1,0:T(8,128)(2,1)S(1)}) custom-call(bf16[1024,1024]{1,0:T(8,128)(2,1)S(1)} %multiply_convert_fusion.refs_0_, bf16[256,512]{1,0:T(8,128)(2,1)S(1)} %convolution_convert_fusion.2.refs_1_, bf16[16,256]{1,0:T(8,128)(2,1)S(1)} %broadcast_in_dim.3.refs_2_), custom_call_target="tpu_custom_call" | custom-call | tf_op jit(solution)/shard_map/sum_left/pallas_call | solution.py:223
  216.6 0.0 copy-start.4
  216.6 1.3 copy-done.4
  217.9 0.6 slice_reduce_fusion
  219.9 0.0 copy-start.1
  219.9 0.2 constant_dynamic-update-slice_fusion.1
  220.1 1.4 copy-done.1
  221.5 0.0 copy-start.8
  221.5 0.0 copy-start.10
  221.5 0.2 constant_dynamic-update-slice_fusion
  221.7 1.4 copy-done.8
  223.1 0.3 copy-done.10
  223.3 0.0 copy-start.5
  223.3 3.7 %multiply_subtract_fusion.1 = f32[512,1024]{1,0:T(8,128)} fusion(f32[512,1024]{1,0:T(8,128)S(1)} %copy-done.8, bf16[2048,1024]{1,0:T(8,128)(2,1)S(1)} %constant_dynamic-update-slice_fusion, f32[]{:T(128)S(6)} %mul.64, bf16[1024,512]{1,0:T(8,128)(2,1)S(1)} %copy-done.10, bf16[1024,512]{1,0:T(8,128)(2,1)S(1)} %gather_acts.1), kind=kOutput, calls=%fused_computation.12 | convolution fusion | flops 2152726528 | bytes 10485764 | tf_op jit(solution)/shard_map/dot_general | solution.py:393
  227.0 0.0 copy-done.5
  227.0 3.7 %multiply_subtract_fusion = f32[512,1024]{1,0:T(8,128)} fusion(f32[512,1024]{1,0:T(8,128)S(1)} %copy-done.8, bf16[2048,1024]{1,0:T(8,128)(2,1)S(1)} %constant_dynamic-update-slice_fusion, bf16[2048,512]{1,0:T(8,128)(2,1)S(1)} %copy-done.5, f32[]{:T(128)S(6)} %mul.67, f32[]{:T(128)S(6)} %mul.64, bf16[1024,512]{1,0:T(8,128)(2,1)S(1)} %copy-done.10, ...), kind=kOutput, calls=%fused_computation.10 | convolution fusion | flops 2156920832 | bytes 12582920 | tf_op jit(solution)/shard_map/dot_general | solution.py:393
  (21 shorter events, 0.3 us)
Async XLA Ops:
  7.2 2.9 %copy-start.3 = (bf16[128,512]{1,0:T(8,128)(2,1)S(1)}, bf16[128,512]{1,0:T(8,128)(2,1)}, u32[]{:S(2)}) copy-start(bf16[128,512]{1,0:T(8,128)(2,1)} %refs_0_.1) | copy-start | bytes 393220
  7.2 123.2 %all-gather.2.cloned.1.call-start = ((), (), s32[]{:S(2)}) async-start(), calls=%async_computation | async-start | bytes 9437184 | tf_op jit(solution)/shard_map/all_gather | solution.py:404
  10.1 14.5 %copy-start.7 = (bf16[512,1024]{1,0:T(8,128)(2,1)S(1)}, bf16[512,1024]{1,0:T(8,128)(2,1)}, u32[]{:S(2)}) copy-start(bf16[512,1024]{1,0:T(8,128)(2,1)} %convert_element_type.50) | copy-start | bytes 3145732
  24.5 49.2 %copy-start.6 = (bf16[8192,896]{1,0:T(8,128)(2,1)S(1)}, bf16[8192,896]{1,0:T(8,128)(2,1)}, u32[]{:S(2)}) copy-start(bf16[8192,896]{1,0:T(8,128)(2,1)} %param.5) | copy-start | bytes 44040196
  73.4 0.9 copy-start.11
  127.7 1.3 copy-start
  129.0 1.3 copy-start.2
  149.5 25.8 %copy-start.9 = (bf16[1024,512]{1,0:T(8,128)(2,1)}, bf16[1024,512]{1,0:T(8,128)(2,1)S(1)}, u32[]{:S(2)}) copy-start(bf16[1024,512]{1,0:T(8,128)(2,1)S(1)} %neg.14) | copy-start | bytes 3145732
  216.6 1.3 copy-start.4
  219.9 1.6 copy-start.1
  221.5 1.6 copy-start.8
  221.5 1.9 copy-start.10
  223.3 3.7 %copy-start.5 = (bf16[2048,512]{1,0:T(8,128)(2,1)S(1)}, bf16[2048,512]{1,0:T(8,128)(2,1)}, u32[]{:S(2)}) copy-start(bf16[2048,512]{1,0:T(8,128)(2,1)} %copy-done.4) | copy-start | bytes 6291460
Sparse Core Ops, SparseCore 0:
  10.2 54.9 all-gather.1
